TPU v7x, 128 devices: a whole 4x4x4 slice. The times are simulated.
128 devices in a mesh: pool: 4 (over z), ka: 32 (over x, y, core).
Axes of the slice: x: 4, y: 4, z: 4, core: 2. Of those that a mesh axis runs over, the one named last changes fastest.
Arguments:
- rates: bfloat16 [32768, 4096], P(('pool', 'ka')), may hold values from -0.09375 to 0.09375
- tile_dest: int32 [32768, 1], P(('pool', 'ka')), may hold values from 0 to 127; in each aligned block of 256 rows (0 to 255, 256 to 511, ...) at most 4 rows name the same one
- tile_row: int32 [32768], P(('pool', 'ka')), may hold values from 0 to 3
- tile_col: int32 [32768], P(('pool', 'ka')), may hold values from 0 to 127
- send_list: int32 [128, 128], P(('pool', 'ka')), may hold values from 0 to 3
- drive: float32 [512, 12288], P(('pool', 'ka')), may hold values from -6 to 6
- tau: float32 [512, 4096], P(('pool', 'ka')), may hold values from 0.2 to 1
Outputs:
- population: float32 [512, 12288], P(('pool', 'ka'))
Inputs may be any that keep to these rules, and one draw needn't show every extreme that they name: `tile_dest`: owner device of the tile's k-row block; among the 256 tiles of one device no owner is named more than 4 times. `tile_col`: names the device that lists the tile's k+q column block for the tile's owner. `send_list`: entry [s, d] is the local k block of device s that owner d reads as column entry s.
All inputs are finite; a program needn't handle non-finite values.
Results may differ from a plain program's by a relative error of at most 0.0025.
Values may be sent and summed in bfloat16 or wider, within the bound.
No kernel may reach another device: no remote copies, remote signals or barrier semaphores. Data moves between devices by JAX's collectives and lax.ppermute only.
A program may use at most 64 MiB of HBM per device.

v0:
```python
import jax
import jax.numpy as jnp
from jax import lax
from jax.sharding import PartitionSpec as P

B = 64
NPT = 64
ITERS = 3


def shards(rates, tile_dest, tile_row, tile_col, send_list, drive, tau):
    pool_size = lax.axis_size("pool")
    ka_size = lax.axis_size("ka")
    members = pool_size * ka_size
    tiles_held = rates.shape[0]
    flat_tile = rates.shape[1]
    kblocks = drive.shape[0]
    plane = B * NPT
    capacity = 2 * tiles_held // members
    all_slots = members * capacity
    owner_of = tile_dest[:, 0]
    owners = jnp.arange(members, dtype=jnp.int32)
    matches = (owner_of[:, None] == owners[None, :]).astype(jnp.int32)
    before = jnp.sum(jnp.cumsum(matches, axis=0) * matches, axis=1) - 1
    target = owner_of * capacity + before
    outgoing = jnp.zeros((all_slots, flat_tile), jnp.bfloat16).at[target].set(rates)
    labels = jnp.stack([tile_row, tile_col], axis=1).astype(jnp.bfloat16)
    out_labels = jnp.zeros((all_slots, 2), jnp.bfloat16).at[target].set(labels)
    incoming, in_labels = (
        lax.all_to_all(outgoing, ("pool", "ka"), split_axis=0, concat_axis=0, tiled=True),
        lax.all_to_all(out_labels, ("pool", "ka"), split_axis=0, concat_axis=0, tiled=True),
    )
    row_ids = in_labels[:, 0].astype(jnp.int32)
    col_ids = in_labels[:, 1].astype(jnp.int32)
    pair_ids = row_ids * members + col_ids
    slab = min(256, all_slots)
    rounds = all_slots // slab

    def add_slab(step, summed):
        begin = step * slab
        piece = lax.dynamic_slice_in_dim(incoming, begin, slab, 0).astype(jnp.float32)
        where_to = lax.dynamic_slice_in_dim(pair_ids, begin, slab, 0)
        return summed.at[where_to].add(piece)

    summed = lax.fori_loop(
        0, rounds, add_slab, jnp.zeros((kblocks * members, flat_tile), jnp.float32)
    )
    operator = summed.astype(jnp.bfloat16).reshape(kblocks, members, B, B)
    drive3 = drive.reshape(kblocks, 3, plane)
    spread = tau.reshape(kblocks, 1, plane)
    listed = send_list[0]
    population = drive3
    for sweep in range(ITERS):
        packed = population.astype(jnp.bfloat16)
        outbound = packed[listed]
        blocks = lax.all_to_all(outbound, ("pool", "ka"), split_axis=0, concat_axis=0, tiled=True)
        count = blocks.shape[1]
        shaped = blocks.reshape(members, count, B, NPT)
        result = jnp.einsum("rjab,jnbp->rnap", operator, shaped, preferred_element_type=jnp.float32)
        totals = result.reshape(kblocks, count, plane)
        population = drive3 + spread * totals
    return population.reshape(kblocks, 3 * plane)


def solution(mesh):
    placed = (
        P(("pool", "ka"), None),
        P(("pool", "ka"), None),
        P(("pool", "ka")),
        P(("pool", "ka")),
        P(("pool", "ka"), None),
        P(("pool", "ka"), None),
        P(("pool", "ka"), None),
    )
    return jax.shard_map(
        shards, mesh=mesh, in_specs=placed, out_specs=P(("pool", "ka"), None), check_vma=False
    )
```

profile of v0, /device:TPU:1, one launch (start us, length us, event | category | flops | bytes accessed | tf_op | source)
XLA Modules:
  0.0 384.9 jit_solution(6961437985431109746)
XLA Ops:
  0.0 0.8 copy.71
  0.8 0.2 fusion.20
  1.1 0.9 fusion.21
  2.0 0.7 compare_select_fusion.1
  2.6 0.7 convert.8
  3.3 0.7 convert.9
  4.0 0.1 copy.73
  4.2 1.2 scatter_custom_fusion.1
  5.4 1.5 copy.75
  6.9 11.5 %all-to-all-start.1 = ((bf16[128,4,2]{1,2,0:T(2,128)(2,1)}), bf16[128,4,2]{1,2,0:T(2,128)(2,1)S(1)}, u32[]{:S(2)}, u32[]{:S(2)}) async-start(bf16[128,4,2]{1,2,0:T(2,128)(2,1)} %copy.75), calls=%async_computation.1 | async-start | bytes 131072 | tf_op jit(solution)/shard_map/all_to_all | solution.py:31
  18.4 0.7 fusion.28
  19.1 1.0 convert_element_type.33
  20.0 0.1 copy.69
  20.1 7.5 %gather_fusion = bf16[128,3,4096]{2,1,0:T(4,128)(2,1)} fusion(bf16[4,3,4096]{2,1,0:T(4,128)(2,1)S(1)} %copy.69, s32[1024]{0:T(1024)S(1)} %pad_clamp_fusion), kind=kCustom, calls=%fused_computation | custom fusion | bytes 6291968 | tf_op jit(solution)/shard_map/gather | solution.py:55
  27.6 0.3 all-to-all-done.1
  28.0 9.9 %all-to-all-start = ((bf16[128,3,4096]{2,1,0:T(4,128)(2,1)}), bf16[128,3,4096]{2,1,0:T(4,128)(2,1)}, u32[]{:S(2)}, u32[]{:S(2)}) async-start(bf16[128,3,4096]{2,1,0:T(4,128)(2,1)} %gather_fusion), calls=%async_computation | async-start | bytes 8388608 | tf_op jit(solution)/shard_map/all_to_all | solution.py:56
  37.9 7.1 %scatter_custom_fusion.2 = bf16[512,4096]{1,0:T(8,128)(2,1)} fusion(s32[256]{0:T(256)S(1)} %bitcast.99, bf16[256,4096]{1,0:T(8,128)(2,1)} %param.9, bf16[]{:T(256)} %constant.49.clone.1), kind=kCustom, calls=%fused_computation.16 | custom fusion | bytes 4194816 | tf_op jit(solution)/shard_map/scatter | solution.py:26
  44.9 7.2 %all_to_all.29 = bf16[128,4,4096]{2,1,0:T(4,128)(2,1)} reshape(bf16[512,4096]{1,0:T(8,128)(2,1)} %scatter_custom_fusion.2) | data formatting | bytes 8388608 | tf_op jit(solution)/shard_map/all_to_all | solution.py:30
  52.2 38.4 %all-to-all-done = bf16[128,3,4096]{2,1,0:T(4,128)(2,1)} async-done(((bf16[128,3,4096]{2,1,0:T(4,128)(2,1)}), bf16[128,3,4096]{2,1,0:T(4,128)(2,1)}, u32[]{:S(2)}, u32[]{:S(2)}) %all-to-all-start) | async-done | bytes 3145760 | tf_op jit(solution)/shard_map/all_to_all | solution.py:56
  90.6 5.5 %all-to-all-start.2 = ((bf16[128,4,4096]{2,1,0:T(4,128)(2,1)}), bf16[128,4,4096]{2,1,0:T(4,128)(2,1)}, u32[]{:S(2)}, u32[]{:S(2)}) async-start(bf16[128,4,4096]{2,1,0:T(4,128)(2,1)} %all_to_all.29), calls=%async_computation.2 | async-start | bytes 8388608 | tf_op jit(solution)/shard_map/all_to_all | solution.py:30
  96.1 0.1 all_to_all.28
  96.2 6.1 %copy.70 = bf16[128,3,4096]{0,2,1:T(8,128)(2,1)S(1)} copy(bf16[128,3,4096]{2,1,0:T(4,128)(2,1)} %all-to-all-done) | data formatting | bytes 6291456 | tf_op jit(solution)/shard_map/all_to_all | solution.py:56
  102.3 46.6 %all-to-all-done.2 = bf16[128,4,4096]{2,1,0:T(4,128)(2,1)} async-done(((bf16[128,4,4096]{2,1,0:T(4,128)(2,1)}), bf16[128,4,4096]{2,1,0:T(4,128)(2,1)}, u32[]{:S(2)}, u32[]{:S(2)}) %all-to-all-start.2) | async-done | bytes 4194336 | tf_op jit(solution)/shard_map/all_to_all | solution.py:30
  148.9 6.9 %all_to_all.31 = bf16[512,4096]{1,0:T(8,128)(2,1)} reshape(bf16[128,4,4096]{2,1,0:T(4,128)(2,1)} %all-to-all-done.2) | data formatting | bytes 8388608 | tf_op jit(solution)/shard_map/all_to_all | solution.py:30
  155.8 4.2 %broadcast_in_dim.22 = f32[512,4096]{1,0:T(8,128)} broadcast(f32[]{:T(128)} %constant.48.clone.1), dimensions={} | broadcast | bytes 8388612 | tf_op jit(solution)/shard_map/broadcast_in_dim | solution.py:46
  160.1 27.6 %while.13 = (s32[]{:T(128)}, f32[512,4096]{1,0:T(8,128)}, s32[512]{0:T(512)S(1)}, bf16[512,4096]{1,0:T(8,128)(2,1)}, s32[]{:T(128)}, /*index=5*/s32[]{:T(128)}, s32[]{:T(128)}, s32[]{:T(128)}) while((s32[]{:T(128)}, f32[512,4096]{1,0:T(8,128)}, s32[512]{0:T(512)S(1)}, bf16[512,4096]{1,0:T(8,128)(2,1)}, s32[]{:T(128)}, /*index=5*/s32[]{:T(128)}, ...), condition=%wide.region_7.8_spmd, body=%wide.region_5.0_spmd.sunk | while | flops 2097926 | bytes 10488459 | solution.py:45
  160.1 0.1 compare_select_fusion.4
  160.2 13.7 %scatter_custom_fusion.9 = f32[512,4096]{1,0:T(8,128)} fusion(f32[512,4096]{1,0:T(8,128)} %get-tuple-element.127, s32[256]{0:T(256)S(1)} %compare_select_fusion.4, bf16[512,4096]{1,0:T(8,128)(2,1)} %get-tuple-element.137, s32[]{:T(128)S(6)} %select_n.42, s32[]{:T(128)} %constant.46.clone.1..sunk), kind=kCustom, calls=%fused_computation.6.clone.1 | custom fusion | flops 2097152 | bytes 10486276 | tf_op jit(solution)/shard_map/while/body/eval_jaxpr/scatter-add | solution.py:43
  173.9 0.1 compare_select_fusion.4
  174.0 13.7 %scatter_custom_fusion.9 = f32[512,4096]{1,0:T(8,128)} fusion(f32[512,4096]{1,0:T(8,128)} %get-tuple-element.127, s32[256]{0:T(256)S(1)} %compare_select_fusion.4, bf16[512,4096]{1,0:T(8,128)(2,1)} %get-tuple-element.137, s32[]{:T(128)S(6)} %select_n.42, s32[]{:T(128)} %constant.46.clone.1..sunk), kind=kCustom, calls=%fused_computation.6.clone.1 | custom fusion | flops 2097152 | bytes 10486276 | tf_op jit(solution)/shard_map/while/body/eval_jaxpr/scatter-add | solution.py:43
  187.7 6.0 %convert_element_type.37 = bf16[512,4096]{1,0:T(8,128)(2,1)} convert(f32[512,4096]{1,0:T(8,128)} %get-tuple-element.84) | non-fusion elementwise | flops 2097152 | bytes 12582912 | tf_op jit(solution)/shard_map/convert_element_type | solution.py:48
  193.7 12.6 %reshape.158 = bf16[4,128,64,64]{3,2,1,0:T(8,128)(2,1)} reshape(bf16[512,4096]{1,0:T(8,128)(2,1)} %convert_element_type.37) | data formatting | bytes 8388608 | tf_op jit(solution)/shard_map/reshape | solution.py:48
  206.3 14.8 %copy.78 = bf16[4,128,64,64]{1,2,3,0:T(8,128)(2,1)} copy(bf16[4,128,64,64]{3,2,1,0:T(8,128)(2,1)} %reshape.158) | data formatting | bytes 8388608 | tf_op jit(solution)/shard_map/reshape | solution.py:48
  221.1 0.0 copy-start
  221.1 0.0 copy-start.1
  221.1 4.8 %fusion.11 = f32[4,3,64,64]{2,3,0,1:T(8,128)} fusion(bf16[128,3,64,64,1]{0,3,2,4,1:T(8,128)(2,1)S(1)} %bitcast.83, bf16[4,128,64,64]{1,2,3,0:T(8,128)(2,1)} %copy.78), kind=kOutput, calls=%fused_computation.18 | convolution fusion | flops 805306368 | bytes 7536640 | tf_op jit(solution)/shard_map/rjab,jnbp->rnap/dot_general | solution.py:59
  225.9 1.2 copy.79
  227.0 0.2 reshape.95
  227.2 0.0 copy-done
  227.2 0.0 copy-done.1
  227.2 0.1 add_convert_fusion.1
  227.3 0.1 copy.80
  227.4 7.7 %gather_fusion.1 = bf16[128,3,4096]{2,1,0:T(4,128)(2,1)} fusion(bf16[4,3,4096]{2,1,0:T(4,128)(2,1)S(1)} %copy.80, s32[1024]{0:T(1024)S(1)} %pad_clamp_fusion), kind=kCustom, calls=%fused_computation.1 | custom fusion | bytes 6291968 | tf_op jit(solution)/shard_map/gather | solution.py:55
  235.1 58.5 %all_to_all.39 = bf16[128,3,4096]{2,1,0:T(4,128)(2,1)} all-to-all(bf16[128,3,4096]{2,1,0:T(4,128)(2,1)} %gather_fusion.1), channel_id=1, replica_groups=mesh['pool'=4,'ka'=32] {'pool','ka'}, dimensions={0} | all-to-all | bytes 6291456 | tf_op jit(solution)/shard_map/all_to_all | solution.py:56
  293.6 6.1 %copy.81 = bf16[128,3,4096]{0,2,1:T(8,128)(2,1)S(1)} copy(bf16[128,3,4096]{2,1,0:T(4,128)(2,1)} %all_to_all.39) | data formatting | bytes 6291456 | tf_op jit(solution)/shard_map/all_to_all | solution.py:56
  299.7 4.7 %fusion.14 = f32[4,3,64,64]{2,3,0,1:T(8,128)} fusion(bf16[128,3,64,64,1]{0,3,2,4,1:T(8,128)(2,1)S(1)} %bitcast.85, bf16[4,128,64,64]{1,2,3,0:T(8,128)(2,1)} %copy.78), kind=kOutput, calls=%fused_computation.19 | convolution fusion | flops 805306368 | bytes 7536640 | tf_op jit(solution)/shard_map/rjab,jnbp->rnap/dot_general | solution.py:59
  304.4 1.2 copy.83
  305.6 0.2 reshape.97
  305.8 0.1 add_convert_fusion
  305.8 0.1 copy.84
  305.9 7.5 %gather_fusion.2 = bf16[128,3,4096]{2,1,0:T(4,128)(2,1)} fusion(bf16[4,3,4096]{2,1,0:T(4,128)(2,1)S(1)} %copy.84, s32[1024]{0:T(1024)S(1)} %pad_clamp_fusion), kind=kCustom, calls=%fused_computation.2 | custom fusion | bytes 6291968 | tf_op jit(solution)/shard_map/gather | solution.py:55
  313.4 58.5 %all_to_all.40 = bf16[128,3,4096]{2,1,0:T(4,128)(2,1)} all-to-all(bf16[128,3,4096]{2,1,0:T(4,128)(2,1)} %gather_fusion.2), channel_id=1, replica_groups=mesh['pool'=4,'ka'=32] {'pool','ka'}, dimensions={0} | all-to-all | bytes 6291456 | tf_op jit(solution)/shard_map/all_to_all | solution.py:56
  371.9 6.1 %copy.85 = bf16[128,3,4096]{0,2,1:T(8,128)(2,1)S(1)} copy(bf16[128,3,4096]{2,1,0:T(4,128)(2,1)} %all_to_all.40) | data formatting | bytes 6291456 | tf_op jit(solution)/shard_map/all_to_all | solution.py:56
  378.0 4.7 %fusion.17 = f32[4,3,64,64]{2,3,0,1:T(8,128)} fusion(bf16[128,3,64,64,1]{0,3,2,4,1:T(8,128)(2,1)S(1)} %bitcast.84, bf16[4,128,64,64]{1,2,3,0:T(8,128)(2,1)} %copy.78), kind=kOutput, calls=%fused_computation.20 | convolution fusion | flops 805306368 | bytes 7536640 | tf_op jit(solution)/shard_map/rjab,jnbp->rnap/dot_general | solution.py:59
  382.7 1.2 copy.87
  383.9 0.2 reshape.99
  384.1 0.7 multiply_add_fusion
  (14 shorter events, 0.2 us)
Async XLA Ops:
  6.9 21.1 %all-to-all-start.1 = ((bf16[128,4,2]{1,2,0:T(2,128)(2,1)}), bf16[128,4,2]{1,2,0:T(2,128)(2,1)S(1)}, u32[]{:S(2)}, u32[]{:S(2)}) async-start(bf16[128,4,2]{1,2,0:T(2,128)(2,1)} %copy.75), calls=%async_computation.1 | async-start | bytes 131072 | tf_op jit(solution)/shard_map/all_to_all | solution.py:31
  28.0 62.6 %all-to-all-start = ((bf16[128,3,4096]{2,1,0:T(4,128)(2,1)}), bf16[128,3,4096]{2,1,0:T(4,128)(2,1)}, u32[]{:S(2)}, u32[]{:S(2)}) async-start(bf16[128,3,4096]{2,1,0:T(4,128)(2,1)} %gather_fusion), calls=%async_computation | async-start | bytes 8388608 | tf_op jit(solution)/shard_map/all_to_all | solution.py:56
  90.6 58.3 %all-to-all-start.2 = ((bf16[128,4,4096]{2,1,0:T(4,128)(2,1)}), bf16[128,4,4096]{2,1,0:T(4,128)(2,1)}, u32[]{:S(2)}, u32[]{:S(2)}) async-start(bf16[128,4,4096]{2,1,0:T(4,128)(2,1)} %all_to_all.29), calls=%async_computation.2 | async-start | bytes 8388608 | tf_op jit(solution)/shard_map/all_to_all | solution.py:30
  221.1 6.1 %copy-start = (f32[4,12288]{1,0:T(4,128)S(1)}, f32[4,12288]{1,0:T(4,128)}, u32[]{:S(2)}) copy-start(f32[4,12288]{1,0:T(4,128)} %param.14) | copy-start | bytes 589828
  221.1 6.1 %copy-start.1 = (f32[4,4096]{1,0:T(4,128)S(1)}, f32[4,4096]{1,0:T(4,128)}, u32[]{:S(2)}) copy-start(f32[4,4096]{1,0:T(4,128)} %param.15) | copy-start | bytes 196612
where the time goes:
time: 387 us; the launch traced here: 385 us
  blocking collectives  117 us (30%)
  local copies, waits for them, and re-layouts  102 us (26%)
  waiting for transfers between devices  85.3 us (22%)
  other arithmetic  39.3 us (10%)
  starting transfers between devices  26.9 us (7%)
  matrix products  14.2 us (4%)
    all_to_all x2, blocking collectives, shards(): lax.all_to_all(outbound, ('pool', 'ka'), split_axis=0, concat_axis=0, til...  117 us
    all_to_all x1, waiting for transfers between devices, shards(): lax.all_to_all(outgoing, ('pool', 'ka'), split_axis=0, concat_axis=0, til...  46.6 us
    all_to_all x1, waiting for transfers between devices, shards(): lax.all_to_all(outbound, ('pool', 'ka'), split_axis=0, concat_axis=0, til...  38.4 us
    scatter-add x2, other arithmetic, add_slab(): return summed.at[where_to].add(piece)  27.4 us
    reshape x2, local copies, waits for them, and re-layouts, shards(): operator = summed.astype(jnp.bfloat16).reshape(kblocks, members, B, B)  27.4 us
    gather x3, local copies, waits for them, and re-layouts, shards(): outbound = packed[listed]  22.7 us
    all_to_all x3, local copies, waits for them, and re-layouts, shards(): lax.all_to_all(outbound, ('pool', 'ka'), split_axis=0, concat_axis=0, til...  18.2 us
    dot_general x3, matrix products, shards(): jnp.einsum('rjab,jnbp->rnap', operator, shaped, preferred_element_type=jn...  14.2 us
  transfers between devices with their start and end apart: 3, of which 3 were waited for; matrix products, arithmetic and copies ran while one was open for 6% of the time, Pallas kernels for 0%

commit v1 on v0

v1 whole, which is shorter than its diff:
```python
import functools

import jax
import jax.numpy as jnp
from jax import lax
from jax.experimental import pallas as pl
from jax.experimental.pallas import tpu as pltpu
from jax.sharding import PartitionSpec as P

ROWS = 32
LANES = 128
HALF = 64
ITERS = 3
CAP = 4
DIRS = 3
AXES = ("pool", "ka")
TILE_ROWS = CAP * ROWS
BLOCK_ROWS = DIRS * ROWS
LABEL_AT = TILE_ROWS + BLOCK_ROWS
FIRST_ROWS = LABEL_AT + 8

VMEM = pltpu.MemorySpace.VMEM
SMEM = pltpu.MemorySpace.SMEM


def vspec():
    return pl.BlockSpec(memory_space=VMEM)


def sspec():
    return pl.BlockSpec(memory_space=SMEM)


def params(mib):
    return pltpu.CompilerParams(vmem_limit_bytes=mib << 20)


def fill_kernel(dest_ref, row_ref, col_ref, sel_ref, rates_ref, drive_ref, out_ref, perm_ref, cnt_ref, lab_ref, pk_ref):
    members = out_ref.shape[0]
    tiles = rates_ref.shape[0]
    lane = lax.broadcasted_iota(jnp.int32, (1, LANES), 1)
    lab_ref[...] = jnp.full(lab_ref.shape, 4 * members, jnp.int32)
    pk_ref[...] = drive_ref[...].astype(jnp.bfloat16)

    def block(d, carry):
        cnt_ref[d] = 0
        out_ref[d, TILE_ROWS:LABEL_AT, :] = pk_ref[sel_ref[d]]
        return carry

    lax.fori_loop(0, members, block, 0, unroll=8)

    def place(i, carry):
        d = dest_ref[i]
        c = cnt_ref[d]
        cnt_ref[d] = c + 1
        where = row_ref[i] * members + col_ref[i]
        lab_ref[d] = jnp.where(lane == c, where, lab_ref[d])
        out_ref[d, pl.ds(pl.multiple_of(c * ROWS, ROWS), ROWS), :] = rates_ref[i]
        return carry

    lax.fori_loop(0, tiles, place, 0, unroll=4)

    sub = lax.broadcasted_iota(jnp.int32, (8, LANES), 0)

    def label(d, carry):
        value = jnp.broadcast_to(lab_ref[d], (8, LANES))
        value = jnp.where(sub == 0, value >> 3, value & 7)
        out_ref[d, LABEL_AT:FIRST_ROWS, :] = value.astype(jnp.float32).astype(jnp.bfloat16)
        return carry

    lax.fori_loop(0, members, label, 0, unroll=4)

    size = perm_ref.shape[0]
    k = lax.broadcasted_iota(jnp.int32, (size, size), 0)
    m = lax.broadcasted_iota(jnp.int32, (size, size), 1)
    want = ((m >> 5) & 3) * LANES + (m >> 8) * HALF + 2 * (m & 31) + ((m >> 7) & 1)
    perm_ref[...] = (k == want).astype(jnp.float32).astype(jnp.bfloat16)


def advance(last, op_ref, x_ref, x_at, sel_ref, drive_ref, tau_ref, out_ref, pk_ref):
    members = x_ref.shape[0]
    kblocks = drive_ref.shape[0]
    depth = members * ROWS
    right = [x_ref[:, x_at + n * ROWS : x_at + (n + 1) * ROWS, :].reshape(depth, LANES) for n in range(DIRS)]
    total = jnp.dot(op_ref[...], jnp.concatenate(right, axis=1), preferred_element_type=jnp.float32)
    low = lax.broadcasted_iota(jnp.int32, (ROWS, LANES), 1) < HALF
    for n in range(DIRS):
        for r in range(kblocks):

            def part(hb, ha):
                at = hb * 256 + r * HALF + ha * ROWS
                return total[at : at + ROWS, n * LANES : (n + 1) * LANES]

            same = jnp.where(low, part(0, 0), part(1, 1))
            other = jnp.where(low, part(0, 1), part(1, 0))
            summed = same + pltpu.roll(other, HALF, 1)
            rows = slice(n * ROWS, (n + 1) * ROWS)
            new = drive_ref[r, rows, :] + tau_ref[r] * summed
            if last:
                out_ref[r, rows, :] = new
            else:
                pk_ref[r, rows, :] = new.astype(jnp.bfloat16)
    if not last:

        def block(d, carry):
            out_ref[d] = pk_ref[sel_ref[d]]
            return carry

        lax.fori_loop(0, members, block, 0, unroll=8)


def first_kernel(sel_ref, x_ref, perm_ref, drive_ref, tau_ref, op_ref, out_ref, acc_ref, lab_ref, at_ref, pk_ref, sem):
    members = x_ref.shape[0]

    def read(s, carry):
        value = x_ref[s, LABEL_AT:FIRST_ROWS, :].astype(jnp.float32)
        lab_ref[pl.ds(s, 1), :] = (value[0:1] * 8.0 + value[1:2]).astype(jnp.int32)
        return carry

    lax.fori_loop(0, members, read, 0, unroll=8)
    copy = pltpu.make_async_copy(lab_ref, at_ref, sem)
    copy.start()
    acc_ref[...] = jnp.zeros_like(acc_ref)
    copy.wait()

    def add(s, carry):
        for c in range(CAP):
            tile = x_ref[s, c * ROWS : (c + 1) * ROWS, :].astype(jnp.float32)
            at = at_ref[s, c]
            acc_ref[at] = acc_ref[at] + tile
        return carry

    lax.fori_loop(0, members, add, 0, unroll=2)

    groups = members // 4
    chunk = 8

    def turn(r, carry):
        for g0 in range(0, groups, chunk):
            parts = [[] for _ in range(4)]
            for g in range(g0, g0 + chunk):
                for q in range(4):
                    parts[q].append(acc_ref[r * members + g * 4 + q].astype(jnp.bfloat16))
            left = jnp.concatenate([jnp.concatenate(p, axis=0) for p in parts], axis=1)
            out = jnp.dot(left, perm_ref[...], preferred_element_type=jnp.float32).astype(jnp.bfloat16)
            for ha in range(2):
                for hb in range(2):
                    at = pl.multiple_of(hb * 256 + r * HALF + ha * ROWS, ROWS)
                    piece = out[:, (ha * 2 + hb) * LANES : (ha * 2 + hb + 1) * LANES]
                    for g in range(chunk):
                        op_ref[pl.ds(at, ROWS), (g0 + g) * LANES : (g0 + g + 1) * LANES] = piece[g * ROWS : (g + 1) * ROWS]
        return carry

    lax.fori_loop(0, 4, turn, 0)
    advance(False, op_ref, x_ref, TILE_ROWS, sel_ref, drive_ref, tau_ref, out_ref, pk_ref)


def step_kernel(last, sel_ref, x_ref, op_ref, drive_ref, tau_ref, out_ref, *scratch):
    advance(last, op_ref, x_ref, 0, sel_ref, drive_ref, tau_ref, out_ref, scratch[0] if scratch else None)


def shards(rates, tile_dest, tile_row, tile_col, send_list, drive, tau):
    members = lax.axis_size("pool") * lax.axis_size("ka")
    tiles = rates.shape[0]
    kblocks = drive.shape[0]
    exchange = functools.partial(lax.all_to_all, axis_name=AXES, split_axis=0, concat_axis=0, tiled=True)
    bf16, f32, i32 = jnp.bfloat16, jnp.float32, jnp.int32
    packed = pltpu.VMEM((kblocks, BLOCK_ROWS, LANES), bf16)

    sel = send_list.reshape(members)
    drive3 = drive.reshape(kblocks, BLOCK_ROWS, LANES)
    tau3 = tau.reshape(kblocks, ROWS, LANES)

    first, perm = pl.pallas_call(
        fill_kernel,
        out_shape=[
            jax.ShapeDtypeStruct((members, FIRST_ROWS, LANES), bf16),
            jax.ShapeDtypeStruct((4 * LANES, 4 * LANES), bf16),
        ],
        in_specs=[sspec()] * 4 + [vspec()] * 2,
        out_specs=[vspec()] * 2,
        scratch_shapes=[pltpu.SMEM((members,), i32), pltpu.VMEM((members, 1, LANES), i32), packed],
        compiler_params=params(16),
        name="fill",
    )(tile_dest[:, 0], tile_row, tile_col, sel, rates.reshape(tiles, ROWS, LANES), drive3)
    first, tau3 = lax.optimization_barrier((first, tau3))
    first = exchange(first)

    operator, send = pl.pallas_call(
        first_kernel,
        out_shape=[
            jax.ShapeDtypeStruct((4 * LANES, members * ROWS), bf16),
            jax.ShapeDtypeStruct((members, BLOCK_ROWS, LANES), bf16),
        ],
        in_specs=[sspec()] + [vspec()] * 4,
        out_specs=[vspec()] * 2,
        scratch_shapes=[
            pltpu.VMEM((kblocks * members + 1, ROWS, LANES), f32),
            pltpu.VMEM((members, LANES), i32),
            pltpu.SMEM((members, LANES), i32),
            packed,
            pltpu.SemaphoreType.DMA(()),
        ],
        compiler_params=params(32),
        name="first",
    )(sel, first, perm, drive3, tau3)

    for sweep in range(1, ITERS):
        last = sweep == ITERS - 1
        shape = (kblocks, BLOCK_ROWS, LANES) if last else (members, BLOCK_ROWS, LANES)
        send = pl.pallas_call(
            functools.partial(step_kernel, last),
            out_shape=jax.ShapeDtypeStruct(shape, f32 if last else bf16),
            in_specs=[sspec()] + [vspec()] * 4,
            out_specs=vspec(),
            scratch_shapes=[] if last else [packed],
            compiler_params=params(20),
            name="step_last" if last else "step",
        )(sel, exchange(send), operator, drive3, tau3)
    return send.reshape(kblocks, BLOCK_ROWS * LANES)


def solution(mesh):
    pair = P(AXES, None)
    placed = (pair, pair, P(AXES), P(AXES), pair, pair, pair)
    return jax.shard_map(shards, mesh=mesh, in_specs=placed, out_specs=pair, check_vma=False)
```

time: 387 us -> 217 us (0.56)
  local copies, waits for them, and re-layouts: 102 us -> 4.71 us
  waiting for transfers between devices: 85.3 us -> 0 us
  blocking collectives: 117 us -> 193 us
  other arithmetic: 39.3 us -> 0 us
  starting transfers between devices: 26.9 us -> 0 us
  Pallas kernels: 0 us -> 19.6 us
  matrix products: 14.2 us -> 0 us
    all_to_all x3 -> x0, waiting for transfers between devices: 85.3 us -> none  [the longest x1 46.6 us: shards(): lax.all_to_all(outgoing, ('pool', 'ka'), split_axis=0, concat_axis=0, til...]
    all_to_all x2 -> x3, blocking collectives: 117 us -> 193 us  [the longest x1 101 us: shards(): first = exchange(first)]
    all_to_all x8 -> x0, local copies, waits for them, and re-layouts: 34 us -> none  [the longest x3 18.2 us: shards(): lax.all_to_all(outbound, ('pool', 'ka'), split_axis=0, concat_axis=0, til...]
    reshape x5 -> x0, local copies, waits for them, and re-layouts: 28 us -> none  [the longest x2 27.4 us: shards(): operator = summed.astype(jnp.bfloat16).reshape(kblocks, members, B, B)]
    scatter-add x2 -> x0, other arithmetic: 27.4 us -> none  [add_slab(): return summed.at[where_to].add(piece)]
    all_to_all x3 -> x0, starting transfers between devices: 26.9 us -> none  [the longest x1 11.5 us: shards(): lax.all_to_all(out_labels, ('pool', 'ka'), split_axis=0, concat_axis=0, t...]
    gather x3 -> x0, local copies, waits for them, and re-layouts: 22.7 us -> none  [shards(): outbound = packed[listed]]
    pallas_call x0 -> x4, Pallas kernels: none -> 19.6 us  [the longest x1 10.7 us: shards(): pl.pallas_call(first_kernel, out_shape=[jax.ShapeDtypeStruct((4 * LANES,...]
  transfers between devices with their start and end apart: 3 -> 0, of which waited for: 3 -> 0; matrix products, arithmetic and copies ran while one was open for 6% -> 0% of each run, Pallas kernels for 0% -> 0%
where the time goes in v1:
time: 217 us
  blocking collectives  193 us (89%)
  Pallas kernels  19.6 us (9%)
  local copies, waits for them, and re-layouts  4.71 us (2%)
    all_to_all x1, blocking collectives, shards(): first = exchange(first)  101 us
    all_to_all x2, blocking collectives, shards(): exchange(send)  91.9 us
    pallas_call x1, Pallas kernels, shards(): pl.pallas_call(first_kernel, out_shape=[jax.ShapeDtypeStruct((4 * LANES,...  10.7 us
    pallas_call x2, Pallas kernels, shards(): pl.pallas_call(functools.partial(step_kernel, last), out_shape=jax.ShapeD...  6.14 us
    unnamed x12, local copies, waits for them, and re-layouts  4.71 us

profile of v1, /device:TPU:1, one launch (start us, length us, event | category | flops | bytes accessed | tf_op | source)
XLA Modules:
  0.0 217.1 jit_solution(15949318923398455903)
XLA Ops:
  0.0 0.0 copy-start
  0.0 0.0 copy-start.3
  0.0 0.0 copy-start.2
  0.0 0.0 copy-start.1
  0.0 0.9 copy.17
  0.9 0.9 copy.16
  1.9 2.1 copy.8
  3.9 0.0 copy-done
  3.9 0.0 copy-done.3
  3.9 0.0 copy-done.2
  4.0 0.0 copy-done.1
  4.0 2.8 %fill.1 = (bf16[128,232,128]{2,1,0:T(8,128)(2,1)S(1)}, bf16[512,512]{1,0:T(8,128)(2,1)S(1)}) custom-call(s32[256]{0:T(256)S(1)} %bitcast.29, s32[256]{0:T(256)S(1)} %copy-done.2, s32[256]{0:T(256)S(1)} %copy-done.3, s32[128]{0:T(128)S(1)} %bitcast.25, bf16[256,32,128]{2,1,0:T(8,128)(2,1)S(1)} %bitcast.16, f32[4,96,128]{2,1,0:T(8,128)S(1)} %bitcast.17), custom_call_target="tpu_custom_call" | custom-call | tf_op jit(solution)/shard_map/fill/pallas_call | solution.py:174
  6.8 100.8 %all_to_all.15.x_ref = bf16[128,232,128]{2,1,0:T(8,128)(2,1)S(1)} all-to-all(bf16[128,232,128]{2,1,0:T(8,128)(2,1)S(1)} %get-tuple-element.12), channel_id=1, replica_groups=mesh['pool'=4,'ka'=32] {'pool','ka'}, dimensions={0} | all-to-all | bytes 15204352 | tf_op jit(solution)/shard_map/all_to_all | solution.py:187
  107.6 10.7 %first.1 = (bf16[512,4096]{1,0:T(8,128)(2,1)S(1)}, bf16[128,96,128]{2,1,0:T(8,128)(2,1)S(1)}) custom-call(s32[128]{0:T(128)S(1)} %bitcast.26, bf16[128,232,128]{2,1,0:T(8,128)(2,1)S(1)} %all_to_all.15.x_ref, bf16[512,512]{1,0:T(8,128)(2,1)S(1)} %get-tuple-element.13.perm_ref, f32[4,96,128]{2,1,0:T(8,128)S(1)} %bitcast.18, f32[4,32,128]{2,1,0:T(8,128)S(1)} %bitcast.21), custom_call_target="tpu_custom_call" | custom-call | tf_op jit(solution)/shard_map/first/pallas_call | solution.py:189
  118.3 46.3 %all_to_all.16.x_ref = bf16[128,96,128]{2,1,0:T(8,128)(2,1)S(1)} all-to-all(bf16[128,96,128]{2,1,0:T(8,128)(2,1)S(1)} %get-tuple-element.15), channel_id=1, replica_groups=mesh['pool'=4,'ka'=32] {'pool','ka'}, dimensions={0} | all-to-all | bytes 6291456 | tf_op jit(solution)/shard_map/all_to_all | solution.py:219
  164.6 3.2 %step.1 = bf16[128,96,128]{2,1,0:T(8,128)(2,1)S(1)} custom-call(s32[128]{0:T(128)S(1)} %bitcast.27, bf16[128,96,128]{2,1,0:T(8,128)(2,1)S(1)} %all_to_all.16.x_ref, bf16[512,4096]{1,0:T(8,128)(2,1)S(1)} %get-tuple-element.16.op_ref, f32[4,96,128]{2,1,0:T(8,128)S(1)} %bitcast.19, f32[4,32,128]{2,1,0:T(8,128)S(1)} %bitcast.22), custom_call_target="tpu_custom_call" | custom-call | tf_op jit(solution)/shard_map/step/pallas_call | solution.py:211
  167.8 45.6 %all_to_all.17.x_ref = bf16[128,96,128]{2,1,0:T(8,128)(2,1)S(1)} all-to-all(bf16[128,96,128]{2,1,0:T(8,128)(2,1)S(1)} %step.1), channel_id=1, replica_groups=mesh['pool'=4,'ka'=32] {'pool','ka'}, dimensions={0} | all-to-all | bytes 6291456 | tf_op jit(solution)/shard_map/all_to_all | solution.py:219
  213.4 2.9 %step_last.1 = f32[4,96,128]{2,1,0:T(8,128)S(1)} custom-call(s32[128]{0:T(128)S(1)} %bitcast.28, bf16[128,96,128]{2,1,0:T(8,128)(2,1)S(1)} %all_to_all.17.x_ref, bf16[512,4096]{1,0:T(8,128)(2,1)S(1)} %get-tuple-element.16.op_ref, f32[4,96,128]{2,1,0:T(8,128)S(1)} %bitcast.20, f32[4,32,128]{2,1,0:T(8,128)S(1)} %bitcast.23), custom_call_target="tpu_custom_call" | custom-call | tf_op jit(solution)/shard_map/step_last/pallas_call | solution.py:211
  216.3 0.8 copy.15
Async XLA Ops:
  0.0 3.9 %copy-start = (s32[1,128]{1,0:T(1,128)S(1)}, s32[1,128]{1,0:T(1,128)}, u32[]{:S(2)}) copy-start(s32[1,128]{1,0:T(1,128)} %param.11) | copy-start | bytes 1540
  0.0 3.9 %copy-start.3 = (s32[256]{0:T(256)S(1)}, s32[256]{0:T(256)}, u32[]{:S(2)}) copy-start(s32[256]{0:T(256)} %col_ref.1) | copy-start | bytes 3076
  0.0 3.9 %copy-start.2 = (s32[256]{0:T(256)S(1)}, s32[256]{0:T(256)}, u32[]{:S(2)}) copy-start(s32[256]{0:T(256)} %row_ref.1) | copy-start | bytes 3076
  0.0 3.9 %copy-start.1 = (s32[256,1]{0,1:T(1,128)S(1)}, s32[256,1]{0,1:T(1,128)}, u32[]{:S(2)}) copy-start(s32[256,1]{0,1:T(1,128)} %param.8) | copy-start | bytes 3076

commit v2 on v1

--- a/solution.py
+++ b/solution.py
@@ -35,12 +35,34 @@
     return pltpu.CompilerParams(vmem_limit_bytes=mib << 20)
 
 
-def fill_kernel(dest_ref, row_ref, col_ref, sel_ref, rates_ref, drive_ref, out_ref, perm_ref, cnt_ref, lab_ref, pk_ref):
+def turned(value):
+    return pltpu.roll(value, HALF, 1)
+
+
+def fill_kernel(
+    dest_ref, row_ref, col_ref, sel_ref, rates_ref, drive_ref, tau_ref, out_ref, perm_ref, du_ref, tu_ref, cnt_ref, lab_ref, pk_ref, nat_ref
+):
     members = out_ref.shape[0]
     tiles = rates_ref.shape[0]
+    kblocks = drive_ref.shape[0]
     lane = lax.broadcasted_iota(jnp.int32, (1, LANES), 1)
+    low = lax.broadcasted_iota(jnp.int32, (ROWS, LANES), 1) < HALF
     lab_ref[...] = jnp.full(lab_ref.shape, 4 * members, jnp.int32)
-    pk_ref[...] = drive_ref[...].astype(jnp.bfloat16)
+
+    for k in range(kblocks):
+        for c in range(BLOCK_ROWS):
+            nat_ref[k, c : c + 1, :] = drive_ref[k : k + 1, c * LANES : (c + 1) * LANES]
+        for c in range(ROWS):
+            nat_ref[k, BLOCK_ROWS + c : BLOCK_ROWS + c + 1, :] = tau_ref[k : k + 1, c * LANES : (c + 1) * LANES]
+    for k in range(kblocks):
+        n0, n1, n2, t = (nat_ref[k, n * ROWS : (n + 1) * ROWS, :] for n in range(DIRS + 1))
+        du_ref[k, 0:ROWS, :] = jnp.where(low, n0, turned(n1))
+        du_ref[k, ROWS : 2 * ROWS, :] = jnp.where(low, turned(n0), n1)
+        du_ref[k, 2 * ROWS :, :] = n2
+        tu_ref[k, 0:ROWS, :] = jnp.where(low, t, turned(t))
+        tu_ref[k, ROWS : 2 * ROWS, :] = jnp.where(low, turned(t), t)
+        tu_ref[k, 2 * ROWS :, :] = t
+    pk_ref[...] = du_ref[...].astype(jnp.bfloat16)
 
     def block(d, carry):
         cnt_ref[d] = 0
@@ -71,39 +93,55 @@
     lax.fori_loop(0, members, label, 0, unroll=4)
 
     size = perm_ref.shape[0]
-    k = lax.broadcasted_iota(jnp.int32, (size, size), 0)
-    m = lax.broadcasted_iota(jnp.int32, (size, size), 1)
+    m = lax.broadcasted_iota(jnp.int32, (1, size), 1)
     want = ((m >> 5) & 3) * LANES + (m >> 8) * HALF + 2 * (m & 31) + ((m >> 7) & 1)
-    perm_ref[...] = (k == want).astype(jnp.float32).astype(jnp.bfloat16)
-
-
-def advance(last, op_ref, x_ref, x_at, sel_ref, drive_ref, tau_ref, out_ref, pk_ref):
+    k = lax.broadcasted_iota(jnp.int32, (ROWS, size), 0)
+    for at in range(0, size, ROWS):
+        perm_ref[at : at + ROWS, :] = (k == want - at).astype(jnp.float32).astype(jnp.bfloat16)
+
+
+def advance(last, op_ref, x_ref, x_at, sel_ref, drive_ref, tau_ref, out_ref, new_ref):
     members = x_ref.shape[0]
     kblocks = drive_ref.shape[0]
     depth = members * ROWS
-    right = [x_ref[:, x_at + n * ROWS : x_at + (n + 1) * ROWS, :].reshape(depth, LANES) for n in range(DIRS)]
-    total = jnp.dot(op_ref[...], jnp.concatenate(right, axis=1), preferred_element_type=jnp.float32)
+
+    def part(index):
+        return x_ref[:, x_at + index * ROWS : x_at + (index + 1) * ROWS, :].reshape(depth, LANES)
+
+    third = part(2)
+    sums = [
+        jnp.dot(
+            op_ref[h * 256 : (h + 1) * 256, :],
+            jnp.concatenate([part(h), third], axis=1),
+            preferred_element_type=jnp.float32,
+        )
+        for h in range(2)
+    ]
+    both = sums[0][:, :LANES] + sums[1][:, :LANES]
     low = lax.broadcasted_iota(jnp.int32, (ROWS, LANES), 1) < HALF
-    for n in range(DIRS):
-        for r in range(kblocks):
-
-            def part(hb, ha):
-                at = hb * 256 + r * HALF + ha * ROWS
-                return total[at : at + ROWS, n * LANES : (n + 1) * LANES]
-
-            same = jnp.where(low, part(0, 0), part(1, 1))
-            other = jnp.where(low, part(0, 1), part(1, 0))
-            summed = same + pltpu.roll(other, HALF, 1)
-            rows = slice(n * ROWS, (n + 1) * ROWS)
-            new = drive_ref[r, rows, :] + tau_ref[r] * summed
-            if last:
-                out_ref[r, rows, :] = new
-            else:
-                pk_ref[r, rows, :] = new.astype(jnp.bfloat16)
-    if not last:
+    for r in range(kblocks):
+        at = r * HALF
+        pair = drive_ref[r, : 2 * ROWS, :] + tau_ref[r, : 2 * ROWS, :] * both[at : at + HALF]
+        s00, s01 = (sums[0][at + h * ROWS : at + (h + 1) * ROWS, LANES:] for h in range(2))
+        s10, s11 = (sums[1][at + h * ROWS : at + (h + 1) * ROWS, LANES:] for h in range(2))
+        one = jnp.where(low, s00, s11) + turned(jnp.where(low, s01, s10))
+        one = drive_ref[r, 2 * ROWS :, :] + tau_ref[r, 2 * ROWS :, :] * one
+        if last:
+            even, odd = pair[:ROWS], pair[ROWS:]
+            new_ref[r, 0:ROWS, :] = jnp.where(low, even, turned(odd))
+            new_ref[r, ROWS : 2 * ROWS, :] = jnp.where(low, turned(even), odd)
+            new_ref[r, 2 * ROWS :, :] = one
+        else:
+            new_ref[r, : 2 * ROWS, :] = pair.astype(jnp.bfloat16)
+            new_ref[r, 2 * ROWS :, :] = one.astype(jnp.bfloat16)
+    if last:
+        for k in range(kblocks):
+            for c in range(BLOCK_ROWS):
+                out_ref[k : k + 1, c * LANES : (c + 1) * LANES] = new_ref[k, c : c + 1, :]
+    else:
 
         def block(d, carry):
-            out_ref[d] = pk_ref[sel_ref[d]]
+            out_ref[d] = new_ref[sel_ref[d]]
             return carry
 
         lax.fori_loop(0, members, block, 0, unroll=8)
@@ -124,10 +162,14 @@
     copy.wait()
 
     def add(s, carry):
+        ats = [at_ref[s, c] for c in range(CAP)]
+        tiles = [x_ref[s, c * ROWS : (c + 1) * ROWS, :].astype(jnp.float32) for c in range(CAP)]
+        olds = [acc_ref[at] for at in ats]
         for c in range(CAP):
-            tile = x_ref[s, c * ROWS : (c + 1) * ROWS, :].astype(jnp.float32)
-            at = at_ref[s, c]
-            acc_ref[at] = acc_ref[at] + tile
+            value = olds[c] + tiles[c]
+            for e in range(c):
+                value = value + jnp.where(ats[e] == ats[c], tiles[e], 0.0)
+            acc_ref[ats[c]] = value
         return carry
 
     lax.fori_loop(0, members, add, 0, unroll=2)
@@ -155,8 +197,8 @@
     advance(False, op_ref, x_ref, TILE_ROWS, sel_ref, drive_ref, tau_ref, out_ref, pk_ref)
 
 
-def step_kernel(last, sel_ref, x_ref, op_ref, drive_ref, tau_ref, out_ref, *scratch):
-    advance(last, op_ref, x_ref, 0, sel_ref, drive_ref, tau_ref, out_ref, scratch[0] if scratch else None)
+def step_kernel(last, sel_ref, x_ref, op_ref, drive_ref, tau_ref, out_ref, new_ref):
+    advance(last, op_ref, x_ref, 0, sel_ref, drive_ref, tau_ref, out_ref, new_ref)
 
 
 def shards(rates, tile_dest, tile_row, tile_col, send_list, drive, tau):
@@ -165,25 +207,28 @@
     kblocks = drive.shape[0]
     exchange = functools.partial(lax.all_to_all, axis_name=AXES, split_axis=0, concat_axis=0, tiled=True)
     bf16, f32, i32 = jnp.bfloat16, jnp.float32, jnp.int32
-    packed = pltpu.VMEM((kblocks, BLOCK_ROWS, LANES), bf16)
-
+    held = (kblocks, BLOCK_ROWS, LANES)
     sel = send_list.reshape(members)
-    drive3 = drive.reshape(kblocks, BLOCK_ROWS, LANES)
-    tau3 = tau.reshape(kblocks, ROWS, LANES)
-
-    first, perm = pl.pallas_call(
+
+    first, perm, drive_u, tau_u = pl.pallas_call(
         fill_kernel,
         out_shape=[
             jax.ShapeDtypeStruct((members, FIRST_ROWS, LANES), bf16),
             jax.ShapeDtypeStruct((4 * LANES, 4 * LANES), bf16),
-        ],
-        in_specs=[sspec()] * 4 + [vspec()] * 2,
-        out_specs=[vspec()] * 2,
-        scratch_shapes=[pltpu.SMEM((members,), i32), pltpu.VMEM((members, 1, LANES), i32), packed],
+            jax.ShapeDtypeStruct(held, f32),
+            jax.ShapeDtypeStruct(held, f32),
+        ],
+        in_specs=[sspec()] * 4 + [vspec()] * 3,
+        out_specs=[vspec()] * 4,
+        scratch_shapes=[
+            pltpu.SMEM((members,), i32),
+            pltpu.VMEM((members, 1, LANES), i32),
+            pltpu.VMEM(held, bf16),
+            pltpu.VMEM((kblocks, BLOCK_ROWS + ROWS, LANES), f32),
+        ],
         compiler_params=params(16),
         name="fill",
-    )(tile_dest[:, 0], tile_row, tile_col, sel, rates.reshape(tiles, ROWS, LANES), drive3)
-    first, tau3 = lax.optimization_barrier((first, tau3))
+    )(tile_dest[:, 0], tile_row, tile_col, sel, rates.reshape(tiles, ROWS, LANES), drive, tau)
     first = exchange(first)
 
     operator, send = pl.pallas_call(
@@ -198,26 +243,25 @@
             pltpu.VMEM((kblocks * members + 1, ROWS, LANES), f32),
             pltpu.VMEM((members, LANES), i32),
             pltpu.SMEM((members, LANES), i32),
-            packed,
+            pltpu.VMEM(held, bf16),
             pltpu.SemaphoreType.DMA(()),
         ],
         compiler_params=params(32),
         name="first",
-    )(sel, first, perm, drive3, tau3)
+    )(sel, first, perm, drive_u, tau_u)
 
     for sweep in range(1, ITERS):
         last = sweep == ITERS - 1
-        shape = (kblocks, BLOCK_ROWS, LANES) if last else (members, BLOCK_ROWS, LANES)
         send = pl.pallas_call(
             functools.partial(step_kernel, last),
-            out_shape=jax.ShapeDtypeStruct(shape, f32 if last else bf16),
+            out_shape=jax.ShapeDtypeStruct(drive.shape if last else send.shape, f32 if last else bf16),
             in_specs=[sspec()] + [vspec()] * 4,
             out_specs=vspec(),
-            scratch_shapes=[] if last else [packed],
+            scratch_shapes=[pltpu.VMEM(held, f32 if last else bf16)],
             compiler_params=params(20),
             name="step_last" if last else "step",
-        )(sel, exchange(send), operator, drive3, tau3)
-    return send.reshape(kblocks, BLOCK_ROWS * LANES)
+        )(sel, exchange(send), operator, drive_u, tau_u)
+    return send
 
 
 def solution(mesh):

time: 217 us -> 212 us (0.977)
  local copies, waits for them, and re-layouts: 4.71 us -> 2.14 us
  Pallas kernels: 19.6 us -> 17.1 us
    unnamed x12 -> x13, local copies, waits for them, and re-layouts: 4.71 us -> 2.14 us
where the time goes in v2:
time: 212 us; the launch traced here: 211 us
  blocking collectives  192 us (91%)
  Pallas kernels  17.1 us (8%)
  local copies, waits for them, and re-layouts  2.14 us (1%)
    all_to_all x1, blocking collectives, shards(): first = exchange(first)  101 us
    all_to_all x2, blocking collectives, shards(): exchange(send)  91.2 us
    pallas_call x1, Pallas kernels, shards(): pl.pallas_call(first_kernel, out_shape=[jax.ShapeDtypeStruct((4 * LANES,...  9.31 us
    pallas_call x2, Pallas kernels, shards(): pl.pallas_call(functools.partial(step_kernel, last), out_shape=jax.ShapeD...  4.76 us

profile of v2, /device:TPU:1, one launch (start us, length us, event | category | flops | bytes accessed | tf_op | source)
XLA Modules:
  0.0 211.4 jit_solution(8984428716342391722)
XLA Ops:
  0.0 0.0 copy-start.1
  0.0 0.0 copy-start
  0.0 0.0 copy-start.2
  0.0 0.0 copy-start.5
  0.0 0.0 copy-start.4
  0.0 0.0 copy-start.3
  0.0 2.1 %copy.8 = bf16[32,8,32,128]{3,2,1,0:T(8,128)(2,1)S(1)} copy(bf16[32,8,32,128]{3,1,2,0:T(8,128)(2,1)} %bitcast.10) | data formatting | bytes 4194304
  2.2 0.0 copy-done.1
  2.2 0.0 copy-done
  2.2 0.0 copy-done.2
  2.2 0.0 copy-done.5
  2.2 0.0 copy-done.4
  2.2 0.0 copy-done.3
  2.2 3.1 %fill.1 = (bf16[128,232,128]{2,1,0:T(8,128)(2,1)S(1)}, bf16[512,512]{1,0:T(8,128)(2,1)S(1)}, f32[4,96,128]{2,1,0:T(8,128)S(1)}, f32[4,96,128]{2,1,0:T(8,128)S(1)}) custom-call(s32[256]{0:T(256)S(1)} %bitcast.9, s32[256]{0:T(256)S(1)} %copy-done.4, s32[256]{0:T(256)S(1)} %copy-done.5, s32[128]{0:T(128)S(1)} %bitcast.5, bf16[256,32,128]{2,1,0:T(8,128)(2,1)S(1)} %bitcast.4, ...), custom_call_target="tpu_custom_call" | custom-call | tf_op jit(solution)/shard_map/fill/pallas_call | solution.py:213
  5.3 100.8 %all_to_all.15.x_ref = bf16[128,232,128]{2,1,0:T(8,128)(2,1)S(1)} all-to-all(bf16[128,232,128]{2,1,0:T(8,128)(2,1)S(1)} %get-tuple-element.11), channel_id=1, replica_groups=mesh['pool'=4,'ka'=32] {'pool','ka'}, dimensions={0} | all-to-all | bytes 15204352 | tf_op jit(solution)/shard_map/all_to_all | solution.py:232
  106.1 9.3 %first.1 = (bf16[512,4096]{1,0:T(8,128)(2,1)S(1)}, bf16[128,96,128]{2,1,0:T(8,128)(2,1)S(1)}) custom-call(s32[128]{0:T(128)S(1)} %bitcast.6, bf16[128,232,128]{2,1,0:T(8,128)(2,1)S(1)} %all_to_all.15.x_ref, bf16[512,512]{1,0:T(8,128)(2,1)S(1)} %get-tuple-element.12.perm_ref, f32[4,96,128]{2,1,0:T(8,128)S(1)} %get-tuple-element.13.drive_ref, ...), custom_call_target="tpu_custom_call" | custom-call | tf_op jit(solution)/shard_map/first/pallas_call | solution.py:234
  115.4 45.6 %all_to_all.16.x_ref = bf16[128,96,128]{2,1,0:T(8,128)(2,1)S(1)} all-to-all(bf16[128,96,128]{2,1,0:T(8,128)(2,1)S(1)} %get-tuple-element.15), channel_id=1, replica_groups=mesh['pool'=4,'ka'=32] {'pool','ka'}, dimensions={0} | all-to-all | bytes 6291456 | tf_op jit(solution)/shard_map/all_to_all | solution.py:263
  161.0 2.1 %step.1 = bf16[128,96,128]{2,1,0:T(8,128)(2,1)S(1)} custom-call(s32[128]{0:T(128)S(1)} %bitcast.7, bf16[128,96,128]{2,1,0:T(8,128)(2,1)S(1)} %all_to_all.16.x_ref, bf16[512,4096]{1,0:T(8,128)(2,1)S(1)} %get-tuple-element.16.op_ref, f32[4,96,128]{2,1,0:T(8,128)S(1)} %get-tuple-element.13.drive_ref, f32[4,96,128]{2,1,0:T(8,128)S(1)} %get-tuple-element.14.tau_ref), custom_call_target="tpu_custom_call" | custom-call | tf_op jit(solution)/shard_map/step/pallas_call | solution.py:255
  163.1 45.6 %all_to_all.17.x_ref = bf16[128,96,128]{2,1,0:T(8,128)(2,1)S(1)} all-to-all(bf16[128,96,128]{2,1,0:T(8,128)(2,1)S(1)} %step.1), channel_id=1, replica_groups=mesh['pool'=4,'ka'=32] {'pool','ka'}, dimensions={0} | all-to-all | bytes 6291456 | tf_op jit(solution)/shard_map/all_to_all | solution.py:263
  208.7 2.6 %step_last.1 = f32[4,12288]{1,0:T(4,128)} custom-call(s32[128]{0:T(128)S(1)} %bitcast.8, bf16[128,96,128]{2,1,0:T(8,128)(2,1)S(1)} %all_to_all.17.x_ref, bf16[512,4096]{1,0:T(8,128)(2,1)S(1)} %get-tuple-element.16.op_ref, f32[4,96,128]{2,1,0:T(8,128)S(1)} %get-tuple-element.13.drive_ref, f32[4,96,128]{2,1,0:T(8,128)S(1)} %get-tuple-element.14.tau_ref), custom_call_target="tpu_custom_call" | custom-call | tf_op jit(solution)/shard_map/step_last/pallas_call | solution.py:255
Async XLA Ops:
  0.0 2.2 %copy-start.1 = (f32[4,4096]{1,0:T(4,128)S(1)}, f32[4,4096]{1,0:T(4,128)}, u32[]{:S(2)}) copy-start(f32[4,4096]{1,0:T(4,128)} %tau_ref.1) | copy-start | bytes 196612
  0.0 2.2 %copy-start = (f32[4,12288]{1,0:T(4,128)S(1)}, f32[4,12288]{1,0:T(4,128)}, u32[]{:S(2)}) copy-start(f32[4,12288]{1,0:T(4,128)} %drive_ref.1) | copy-start | bytes 589828
  0.0 2.2 %copy-start.2 = (s32[1,128]{1,0:T(1,128)S(1)}, s32[1,128]{1,0:T(1,128)}, u32[]{:S(2)}) copy-start(s32[1,128]{1,0:T(1,128)} %param.11) | copy-start | bytes 1540
  0.0 2.2 %copy-start.5 = (s32[256]{0:T(256)S(1)}, s32[256]{0:T(256)}, u32[]{:S(2)}) copy-start(s32[256]{0:T(256)} %col_ref.1) | copy-start | bytes 3076
  0.0 2.2 %copy-start.4 = (s32[256]{0:T(256)S(1)}, s32[256]{0:T(256)}, u32[]{:S(2)}) copy-start(s32[256]{0:T(256)} %row_ref.1) | copy-start | bytes 3076
  0.0 2.2 %copy-start.3 = (s32[256,1]{0,1:T(1,128)S(1)}, s32[256,1]{0,1:T(1,128)}, u32[]{:S(2)}) copy-start(s32[256,1]{0,1:T(1,128)} %param.8) | copy-start | bytes 3076

commit v3 on v2

v3 whole, which is shorter than its diff:
```python
import functools

import jax
import jax.numpy as jnp
from jax import lax
from jax.experimental import pallas as pl
from jax.experimental.pallas import tpu as pltpu
from jax.sharding import PartitionSpec as P

ROWS = 32
LANES = 128
HALF = 64
ITERS = 3
CAP = 4
DIRS = 3
AXES = ("pool", "ka")
TILE_ROWS = CAP * ROWS
BLOCK_ROWS = DIRS * ROWS
LABEL_AT = TILE_ROWS + BLOCK_ROWS
FIRST_ROWS = LABEL_AT + 8

VMEM = pltpu.MemorySpace.VMEM
SMEM = pltpu.MemorySpace.SMEM


def vspec():
    return pl.BlockSpec(memory_space=VMEM)


def sspec():
    return pl.BlockSpec(memory_space=SMEM)


def params(mib):
    return pltpu.CompilerParams(vmem_limit_bytes=mib << 20)


def turned(value):
    return pltpu.roll(value, HALF, 1)


def low_half(rows):
    return lax.broadcasted_iota(jnp.int32, (rows, LANES), 1) < HALF


def send_block(k, even, odd, natural, rows_ref, pk_ref):
    low = low_half(ROWS)
    rows_ref[pl.ds(0, ROWS, stride=2), :] = even
    rows_ref[pl.ds(1, ROWS, stride=2), :] = odd
    pk_ref[k, :HALF, :] = rows_ref[...].astype(jnp.bfloat16)
    rows_ref[pl.ds(0, ROWS, stride=2), :] = natural
    rows_ref[pl.ds(1, ROWS, stride=2), :] = turned(natural)
    pk_ref[k, HALF:, :] = jnp.where(low, rows_ref[:ROWS, :], turned(rows_ref[ROWS:, :])).astype(jnp.bfloat16)


def fill_kernel(
    dest_ref, row_ref, col_ref, sel_ref, rates_ref, drive_ref, tau_ref, out_ref, du_ref, tu_ref, cnt_ref, lab_ref, pk_ref, nat_ref, rows_ref
):
    members = out_ref.shape[0]
    tiles = rates_ref.shape[0]
    kblocks = drive_ref.shape[0]
    lane = lax.broadcasted_iota(jnp.int32, (1, LANES), 1)
    low = low_half(ROWS)
    lab_ref[...] = jnp.full(lab_ref.shape, 4 * members, jnp.int32)

    for k in range(kblocks):
        for c in range(BLOCK_ROWS):
            nat_ref[k, c : c + 1, :] = drive_ref[k : k + 1, c * LANES : (c + 1) * LANES]
        for c in range(ROWS):
            nat_ref[k, BLOCK_ROWS + c : BLOCK_ROWS + c + 1, :] = tau_ref[k : k + 1, c * LANES : (c + 1) * LANES]
    for k in range(kblocks):
        n0, n1, n2, t = (nat_ref[k, n * ROWS : (n + 1) * ROWS, :] for n in range(DIRS + 1))
        even = jnp.where(low, n0, turned(n1))
        odd = jnp.where(low, turned(n0), n1)
        du_ref[k, 0:ROWS, :] = even
        du_ref[k, ROWS : 2 * ROWS, :] = odd
        du_ref[k, 2 * ROWS :, :] = n2
        tu_ref[k, 0:ROWS, :] = jnp.where(low, t, turned(t))
        tu_ref[k, ROWS : 2 * ROWS, :] = jnp.where(low, turned(t), t)
        tu_ref[k, 2 * ROWS :, :] = t
        send_block(k, even, odd, n2, rows_ref.at[k], pk_ref)

    def block(d, carry):
        cnt_ref[d] = 0
        out_ref[d, TILE_ROWS:LABEL_AT, :] = pk_ref[sel_ref[d]]
        return carry

    lax.fori_loop(0, members, block, 0, unroll=8)

    def place(i, carry):
        d = dest_ref[i]
        c = cnt_ref[d]
        cnt_ref[d] = c + 1
        where = row_ref[i] * members + col_ref[i]
        lab_ref[d] = jnp.where(lane == c, where, lab_ref[d])
        out_ref[d, pl.ds(pl.multiple_of(c * ROWS, ROWS), ROWS), :] = rates_ref[i]
        return carry

    lax.fori_loop(0, tiles, place, 0, unroll=4)

    sub = lax.broadcasted_iota(jnp.int32, (8, LANES), 0)

    def label(d, carry):
        value = jnp.broadcast_to(lab_ref[d], (8, LANES))
        value = jnp.where(sub == 0, value >> 3, value & 7)
        out_ref[d, LABEL_AT:FIRST_ROWS, :] = value.astype(jnp.float32).astype(jnp.bfloat16)
        return carry

    lax.fori_loop(0, members, label, 0, unroll=4)


def advance(last, op_ref, x_ref, x_at, sel_ref, drive_ref, tau_ref, out_ref, new_ref, rows_ref):
    members = x_ref.shape[0]
    kblocks = drive_ref.shape[0]
    low = low_half(ROWS)
    zero = jnp.zeros((), jnp.bfloat16)
    third = x_ref[:, x_at + HALF : x_at + BLOCK_ROWS, :]
    third = jnp.concatenate([jnp.where(low, third, zero), jnp.where(low, zero, third)], axis=1)
    pair = x_ref[:, x_at : x_at + HALF, :]
    right = jnp.concatenate([v.reshape(members * HALF, LANES) for v in (pair, third)], axis=1)
    total = jnp.dot(op_ref[...], right, preferred_element_type=jnp.float32)
    for r in range(kblocks):
        at = r * HALF
        pair = drive_ref[r, : 2 * ROWS, :] + tau_ref[r, : 2 * ROWS, :] * total[at : at + HALF, :LANES]
        even, odd = pair[:ROWS], pair[ROWS:]
        one = total[at : at + HALF, LANES:]
        one = one + turned(one)
        one = jnp.where(low, one[:ROWS], one[ROWS:])
        one = drive_ref[r, 2 * ROWS :, :] + tau_ref[r, 2 * ROWS :, :] * one
        if last:
            new_ref[r, 0:ROWS, :] = jnp.where(low, even, turned(odd))
            new_ref[r, ROWS : 2 * ROWS, :] = jnp.where(low, turned(even), odd)
            new_ref[r, 2 * ROWS :, :] = one
        else:
            send_block(r, even, odd, one, rows_ref.at[r], new_ref)
    if last:
        for k in range(kblocks):
            for c in range(BLOCK_ROWS):
                out_ref[k : k + 1, c * LANES : (c + 1) * LANES] = new_ref[k, c : c + 1, :]
    else:

        def block(d, carry):
            out_ref[d] = new_ref[sel_ref[d]]
            return carry

        lax.fori_loop(0, members, block, 0, unroll=8)


def first_kernel(sel_ref, x_ref, drive_ref, tau_ref, op_ref, out_ref, acc_ref, lab_ref, at_ref, pk_ref, rows_ref, sem):
    members = x_ref.shape[0]
    kblocks = drive_ref.shape[0]

    def read(s, carry):
        value = x_ref[s, LABEL_AT:FIRST_ROWS, :].astype(jnp.float32)
        lab_ref[pl.ds(s, 1), :] = (value[0:1] * 8.0 + value[1:2]).astype(jnp.int32)
        return carry

    lax.fori_loop(0, members, read, 0, unroll=8)
    copy = pltpu.make_async_copy(lab_ref, at_ref, sem)
    copy.start()
    acc_ref[...] = jnp.zeros_like(acc_ref)
    copy.wait()

    def add(s, carry):
        ats = [at_ref[s, c] for c in range(CAP)]
        olds = [acc_ref[at] for at in ats]
        news = []
        for c in range(CAP):
            old = olds[c]
            for e in range(c):
                old = jnp.where(ats[e] == ats[c], news[e], old)
            news.append(old + x_ref[s, c * ROWS : (c + 1) * ROWS, :].astype(jnp.float32))
        for c in range(CAP):
            acc_ref[ats[c]] = news[c]
        return carry

    lax.fori_loop(0, members, add, 0, unroll=2)

    low = low_half(ROWS)

    def join(r, carry):
        at = pl.multiple_of(r * HALF, HALF)
        for g in range(members // 2):
            a = acc_ref[r * members + 2 * g]
            b = acc_ref[r * members + 2 * g + 1]
            lanes = slice(g * LANES, (g + 1) * LANES)
            op_ref[pl.ds(at, ROWS), lanes] = jnp.where(low, a, turned(b)).astype(jnp.bfloat16)
            op_ref[pl.ds(at + ROWS, ROWS), lanes] = jnp.where(low, turned(a), b).astype(jnp.bfloat16)
        return carry

    lax.fori_loop(0, kblocks, join, 0)
    advance(False, op_ref, x_ref, TILE_ROWS, sel_ref, drive_ref, tau_ref, out_ref, pk_ref, rows_ref)


def step_kernel(last, sel_ref, x_ref, op_ref, drive_ref, tau_ref, out_ref, new_ref, rows_ref):
    advance(last, op_ref, x_ref, 0, sel_ref, drive_ref, tau_ref, out_ref, new_ref, rows_ref)


def shards(rates, tile_dest, tile_row, tile_col, send_list, drive, tau):
    members = lax.axis_size("pool") * lax.axis_size("ka")
    tiles = rates.shape[0]
    kblocks = drive.shape[0]
    exchange = functools.partial(lax.all_to_all, axis_name=AXES, split_axis=0, concat_axis=0, tiled=True)
    bf16, f32, i32 = jnp.bfloat16, jnp.float32, jnp.int32
    held = (kblocks, BLOCK_ROWS, LANES)
    rows = pltpu.VMEM((kblocks, HALF, LANES), f32)
    sel = send_list.reshape(members)

    first, drive_u, tau_u = pl.pallas_call(
        fill_kernel,
        out_shape=[
            jax.ShapeDtypeStruct((members, FIRST_ROWS, LANES), bf16),
            jax.ShapeDtypeStruct(held, f32),
            jax.ShapeDtypeStruct(held, f32),
        ],
        in_specs=[sspec()] * 4 + [vspec()] * 3,
        out_specs=[vspec()] * 3,
        scratch_shapes=[
            pltpu.SMEM((members,), i32),
            pltpu.VMEM((members, 1, LANES), i32),
            pltpu.VMEM(held, bf16),
            pltpu.VMEM((kblocks, BLOCK_ROWS + ROWS, LANES), f32),
            rows,
        ],
        compiler_params=params(16),
        name="fill",
    )(tile_dest[:, 0], tile_row, tile_col, sel, rates.reshape(tiles, ROWS, LANES), drive, tau)
    first = exchange(first)

    operator, send = pl.pallas_call(
        first_kernel,
        out_shape=[
            jax.ShapeDtypeStruct((kblocks * HALF, members * HALF), bf16),
            jax.ShapeDtypeStruct((members, BLOCK_ROWS, LANES), bf16),
        ],
        in_specs=[sspec()] + [vspec()] * 3,
        out_specs=[vspec()] * 2,
        scratch_shapes=[
            pltpu.VMEM((kblocks * members + 1, ROWS, LANES), f32),
            pltpu.VMEM((members, LANES), i32),
            pltpu.SMEM((members, LANES), i32),
            pltpu.VMEM(held, bf16),
            rows,
            pltpu.SemaphoreType.DMA(()),
        ],
        compiler_params=params(32),
        name="first",
    )(sel, first, drive_u, tau_u)

    for sweep in range(1, ITERS):
        last = sweep == ITERS - 1
        send = pl.pallas_call(
            functools.partial(step_kernel, last),
            out_shape=jax.ShapeDtypeStruct(drive.shape if last else send.shape, f32 if last else bf16),
            in_specs=[sspec()] + [vspec()] * 4,
            out_specs=vspec(),
            scratch_shapes=[pltpu.VMEM(held, f32 if last else bf16), rows],
            compiler_params=params(20),
            name="step_last" if last else "step",
        )(sel, exchange(send), operator, drive_u, tau_u)
    return send


def solution(mesh):
    pair = P(AXES, None)
    placed = (pair, pair, P(AXES), P(AXES), pair, pair, pair)
    return jax.shard_map(shards, mesh=mesh, in_specs=placed, out_specs=pair, check_vma=False)
```

time: 212 us -> 210 us (level)
  no operation moved by 1% of the time
where the time goes in v3:
time: 210 us; the launch traced here: 209 us
  blocking collectives  192 us (91%)
  Pallas kernels  15.2 us (7%)
  local copies, waits for them, and re-layouts  2.14 us (1%)
    all_to_all x1, blocking collectives, shards(): first = exchange(first)  101 us
    all_to_all x2, blocking collectives, shards(): exchange(send)  91.2 us
    pallas_call x1, Pallas kernels, shards(): pl.pallas_call(first_kernel, out_shape=[jax.ShapeDtypeStruct((kblocks * H...  7.28 us
    pallas_call x2, Pallas kernels, shards(): pl.pallas_call(functools.partial(step_kernel, last), out_shape=jax.ShapeD...  4.93 us

profile of v3, /device:TPU:1, one launch (start us, length us, event | category | flops | bytes accessed | tf_op | source)
XLA Modules:
  0.0 209.4 jit_solution(17140449209783945243)
XLA Ops:
  0.0 0.0 copy-start.1
  0.0 0.0 copy-start
  0.0 0.0 copy-start.2
  0.0 0.0 copy-start.5
  0.0 0.0 copy-start.4
  0.0 0.0 copy-start.3
  0.0 2.1 %copy.8 = bf16[32,8,32,128]{3,2,1,0:T(8,128)(2,1)S(1)} copy(bf16[32,8,32,128]{3,1,2,0:T(8,128)(2,1)} %bitcast.10) | data formatting | bytes 4194304
  2.2 0.0 copy-done.1
  2.2 0.0 copy-done
  2.2 0.0 copy-done.2
  2.2 0.0 copy-done.5
  2.2 0.0 copy-done.4
  2.2 0.0 copy-done.3
  2.2 3.0 %fill.1 = (bf16[128,232,128]{2,1,0:T(8,128)(2,1)S(1)}, f32[4,96,128]{2,1,0:T(8,128)S(1)}, f32[4,96,128]{2,1,0:T(8,128)S(1)}) custom-call(s32[256]{0:T(256)S(1)} %bitcast.9, s32[256]{0:T(256)S(1)} %copy-done.4, s32[256]{0:T(256)S(1)} %copy-done.5, s32[128]{0:T(128)S(1)} %bitcast.5, bf16[256,32,128]{2,1,0:T(8,128)(2,1)S(1)} %bitcast.4, ...), custom_call_target="tpu_custom_call" | custom-call | tf_op jit(solution)/shard_map/fill/pallas_call | solution.py:209
  5.2 100.8 %all_to_all.15.x_ref = bf16[128,232,128]{2,1,0:T(8,128)(2,1)S(1)} all-to-all(bf16[128,232,128]{2,1,0:T(8,128)(2,1)S(1)} %get-tuple-element.10), channel_id=1, replica_groups=mesh['pool'=4,'ka'=32] {'pool','ka'}, dimensions={0} | all-to-all | bytes 15204352 | tf_op jit(solution)/shard_map/all_to_all | solution.py:228
  106.0 7.3 %first.1 = (bf16[256,8192]{1,0:T(8,128)(2,1)S(1)}, bf16[128,96,128]{2,1,0:T(8,128)(2,1)S(1)}) custom-call(s32[128]{0:T(128)S(1)} %bitcast.6, bf16[128,232,128]{2,1,0:T(8,128)(2,1)S(1)} %all_to_all.15.x_ref, f32[4,96,128]{2,1,0:T(8,128)S(1)} %get-tuple-element.11.drive_ref, f32[4,96,128]{2,1,0:T(8,128)S(1)} %get-tuple-element.12.tau_ref), custom_call_target="tpu_custom_call" | custom-call | tf_op jit(solution)/shard_map/first/pallas_call | solution.py:230
  113.3 45.6 %all_to_all.16.x_ref = bf16[128,96,128]{2,1,0:T(8,128)(2,1)S(1)} all-to-all(bf16[128,96,128]{2,1,0:T(8,128)(2,1)S(1)} %get-tuple-element.13), channel_id=1, replica_groups=mesh['pool'=4,'ka'=32] {'pool','ka'}, dimensions={0} | all-to-all | bytes 6291456 | tf_op jit(solution)/shard_map/all_to_all | solution.py:260
  158.9 2.3 %step.1 = bf16[128,96,128]{2,1,0:T(8,128)(2,1)S(1)} custom-call(s32[128]{0:T(128)S(1)} %bitcast.7, bf16[128,96,128]{2,1,0:T(8,128)(2,1)S(1)} %all_to_all.16.x_ref, bf16[256,8192]{1,0:T(8,128)(2,1)S(1)} %get-tuple-element.14.op_ref, f32[4,96,128]{2,1,0:T(8,128)S(1)} %get-tuple-element.11.drive_ref, f32[4,96,128]{2,1,0:T(8,128)S(1)} %get-tuple-element.12.tau_ref), custom_call_target="tpu_custom_call" | custom-call | tf_op jit(solution)/shard_map/step/pallas_call | solution.py:252
  161.2 45.6 %all_to_all.17.x_ref = bf16[128,96,128]{2,1,0:T(8,128)(2,1)S(1)} all-to-all(bf16[128,96,128]{2,1,0:T(8,128)(2,1)S(1)} %step.1), channel_id=1, replica_groups=mesh['pool'=4,'ka'=32] {'pool','ka'}, dimensions={0} | all-to-all | bytes 6291456 | tf_op jit(solution)/shard_map/all_to_all | solution.py:260
  206.8 2.6 %step_last.1 = f32[4,12288]{1,0:T(4,128)} custom-call(s32[128]{0:T(128)S(1)} %bitcast.8, bf16[128,96,128]{2,1,0:T(8,128)(2,1)S(1)} %all_to_all.17.x_ref, bf16[256,8192]{1,0:T(8,128)(2,1)S(1)} %get-tuple-element.14.op_ref, f32[4,96,128]{2,1,0:T(8,128)S(1)} %get-tuple-element.11.drive_ref, f32[4,96,128]{2,1,0:T(8,128)S(1)} %get-tuple-element.12.tau_ref), custom_call_target="tpu_custom_call" | custom-call | tf_op jit(solution)/shard_map/step_last/pallas_call | solution.py:252
Async XLA Ops:
  0.0 2.2 %copy-start.1 = (f32[4,4096]{1,0:T(4,128)S(1)}, f32[4,4096]{1,0:T(4,128)}, u32[]{:S(2)}) copy-start(f32[4,4096]{1,0:T(4,128)} %tau_ref.1) | copy-start | bytes 196612
  0.0 2.2 %copy-start = (f32[4,12288]{1,0:T(4,128)S(1)}, f32[4,12288]{1,0:T(4,128)}, u32[]{:S(2)}) copy-start(f32[4,12288]{1,0:T(4,128)} %drive_ref.1) | copy-start | bytes 589828
  0.0 2.2 %copy-start.2 = (s32[1,128]{1,0:T(1,128)S(1)}, s32[1,128]{1,0:T(1,128)}, u32[]{:S(2)}) copy-start(s32[1,128]{1,0:T(1,128)} %param.11) | copy-start | bytes 1540
  0.0 2.2 %copy-start.5 = (s32[256]{0:T(256)S(1)}, s32[256]{0:T(256)}, u32[]{:S(2)}) copy-start(s32[256]{0:T(256)} %col_ref.1) | copy-start | bytes 3076
  0.0 2.2 %copy-start.4 = (s32[256]{0:T(256)S(1)}, s32[256]{0:T(256)}, u32[]{:S(2)}) copy-start(s32[256]{0:T(256)} %row_ref.1) | copy-start | bytes 3076
  0.0 2.2 %copy-start.3 = (s32[256,1]{0,1:T(1,128)S(1)}, s32[256,1]{0,1:T(1,128)}, u32[]{:S(2)}) copy-start(s32[256,1]{0,1:T(1,128)} %param.8) | copy-start | bytes 3076

commit v4 on v3

--- a/solution.py
+++ b/solution.py
@@ -54,14 +54,30 @@
 
 
 def fill_kernel(
-    dest_ref, row_ref, col_ref, sel_ref, rates_ref, drive_ref, tau_ref, out_ref, du_ref, tu_ref, cnt_ref, lab_ref, pk_ref, nat_ref, rows_ref
+    dest_ref, sel_ref, dests_ref, tile_rows_ref, cols_ref, rates_ref, drive_ref, tau_ref, out_ref, du_ref, tu_ref,
+    slot_ref, slots_ref, lab_ref, pk_ref, nat_ref, rows_ref, sem,
 ):
     members = out_ref.shape[0]
     tiles = rates_ref.shape[0]
     kblocks = drive_ref.shape[0]
-    lane = lax.broadcasted_iota(jnp.int32, (1, LANES), 1)
+    f32, bf16, i32 = jnp.float32, jnp.bfloat16, jnp.int32
     low = low_half(ROWS)
-    lab_ref[...] = jnp.full(lab_ref.shape, 4 * members, jnp.int32)
+
+    named = (lax.broadcasted_iota(i32, (members, tiles), 0) == dests_ref[...]).astype(f32)
+    i0 = lax.broadcasted_iota(i32, (tiles, tiles), 0)
+    i1 = lax.broadcasted_iota(i32, (tiles, tiles), 1)
+    earlier = jnp.dot(named.astype(bf16), (i0 < i1).astype(f32).astype(bf16), preferred_element_type=f32)
+    slot = jnp.sum(named * earlier, axis=0, keepdims=True).astype(i32)
+    slot_ref[...] = slot
+    copy = pltpu.make_async_copy(slot_ref, slots_ref, sem)
+    copy.start()
+    where = tile_rows_ref[...] * members + cols_ref[...]
+    sub = lax.broadcasted_iota(i32, (LANES, tiles), 0)
+    value = jnp.where(sub < CAP, (where >> 3) - 4 * members // 8, where & 7)
+    value = jnp.where((slot == (sub & (CAP - 1))) & (sub < 2 * CAP), value, 0)
+    lab_ref[...] = lax.dot_general(
+        named.astype(bf16), value.astype(f32).astype(bf16), (((1,), (1,)), ((), ())), preferred_element_type=f32
+    )
 
     for k in range(kblocks):
         for c in range(BLOCK_ROWS):
@@ -81,32 +97,19 @@
         send_block(k, even, odd, n2, rows_ref.at[k], pk_ref)
 
     def block(d, carry):
-        cnt_ref[d] = 0
         out_ref[d, TILE_ROWS:LABEL_AT, :] = pk_ref[sel_ref[d]]
+        out_ref[d, LABEL_AT:FIRST_ROWS, :] = jnp.broadcast_to(lab_ref[pl.ds(d, 1), :], (8, LANES)).astype(bf16)
         return carry
 
     lax.fori_loop(0, members, block, 0, unroll=8)
-
-    def place(i, carry):
-        d = dest_ref[i]
-        c = cnt_ref[d]
-        cnt_ref[d] = c + 1
-        where = row_ref[i] * members + col_ref[i]
-        lab_ref[d] = jnp.where(lane == c, where, lab_ref[d])
-        out_ref[d, pl.ds(pl.multiple_of(c * ROWS, ROWS), ROWS), :] = rates_ref[i]
-        return carry
-
-    lax.fori_loop(0, tiles, place, 0, unroll=4)
-
-    sub = lax.broadcasted_iota(jnp.int32, (8, LANES), 0)
-
-    def label(d, carry):
-        value = jnp.broadcast_to(lab_ref[d], (8, LANES))
-        value = jnp.where(sub == 0, value >> 3, value & 7)
-        out_ref[d, LABEL_AT:FIRST_ROWS, :] = value.astype(jnp.float32).astype(jnp.bfloat16)
-        return carry
-
-    lax.fori_loop(0, members, label, 0, unroll=4)
+    copy.wait()
+
+    def move(i, carry):
+        start = pl.multiple_of(slots_ref[0, i] * ROWS, ROWS)
+        out_ref[dest_ref[i], pl.ds(start, ROWS), :] = rates_ref[i]
+        return carry
+
+    lax.fori_loop(0, tiles, move, 0, unroll=8)
 
 
 def advance(last, op_ref, x_ref, x_at, sel_ref, drive_ref, tau_ref, out_ref, new_ref, rows_ref):
@@ -146,35 +149,60 @@
         lax.fori_loop(0, members, block, 0, unroll=8)
 
 
-def first_kernel(sel_ref, x_ref, drive_ref, tau_ref, op_ref, out_ref, acc_ref, lab_ref, at_ref, pk_ref, rows_ref, sem):
+def first_kernel(sel_ref, x_ref, drive_ref, tau_ref, op_ref, out_ref, acc_ref, raw_ref, lab_ref, at_ref, pk_ref, rows_ref, sem):
     members = x_ref.shape[0]
     kblocks = drive_ref.shape[0]
 
+    none = 4 * members
+
     def read(s, carry):
-        value = x_ref[s, LABEL_AT:FIRST_ROWS, :].astype(jnp.float32)
-        lab_ref[pl.ds(s, 1), :] = (value[0:1] * 8.0 + value[1:2]).astype(jnp.int32)
+        raw_ref[pl.ds(s, 1), :] = x_ref[s, LABEL_AT:FIRST_ROWS, :].astype(jnp.float32)[0:1]
         return carry
 
     lax.fori_loop(0, members, read, 0, unroll=8)
+    raw = raw_ref[...]
+    place = (raw * 8.0 + pltpu.roll(raw, LANES - CAP, 1)).astype(jnp.int32) + none
+    lane = lax.broadcasted_iota(jnp.int32, place.shape, 1)
+    lost = jnp.zeros_like(place)
+    for k in range(1, CAP):
+        again = (place == pltpu.roll(place, LANES - k, 1)) & (lane < CAP - k) & (place < none)
+        lost = jnp.where(again, 1, lost)
+    some = lost
+    for k in range(1, CAP):
+        some = some + pltpu.roll(lost, k, 1)
+    place = jnp.where(lane < CAP, place, jnp.where(lane < 2 * CAP, pltpu.roll(lost, CAP, 1), pltpu.roll(some, CAP + 1, 1)))
+    lab_ref[...] = place
     copy = pltpu.make_async_copy(lab_ref, at_ref, sem)
     copy.start()
     acc_ref[...] = jnp.zeros_like(acc_ref)
     copy.wait()
 
-    def add(s, carry):
-        ats = [at_ref[s, c] for c in range(CAP)]
-        olds = [acc_ref[at] for at in ats]
-        news = []
-        for c in range(CAP):
-            old = olds[c]
-            for e in range(c):
-                old = jnp.where(ats[e] == ats[c], news[e], old)
-            news.append(old + x_ref[s, c * ROWS : (c + 1) * ROWS, :].astype(jnp.float32))
-        for c in range(CAP):
-            acc_ref[ats[c]] = news[c]
-        return carry
-
-    lax.fori_loop(0, members, add, 0, unroll=2)
+    def tile(s, c):
+        return x_ref[s, c * ROWS : (c + 1) * ROWS, :].astype(jnp.float32)
+
+    def repair(s):
+        for c in range(CAP - 1):
+
+            @pl.when(at_ref[s, CAP + c] > 0)
+            def _():
+                at = at_ref[s, c]
+                acc_ref[at] = acc_ref[at] + tile(s, c)
+
+    def add(h, carry):
+        for s in (2 * h, 2 * h + 1):
+            ats = [at_ref[s, c] for c in range(CAP)]
+            news = [acc_ref[ats[c]] + tile(s, c) for c in range(CAP)]
+            for c in range(CAP):
+                acc_ref[ats[c]] = news[c]
+
+        @pl.when(at_ref[2 * h, 2 * CAP] + at_ref[2 * h + 1, 2 * CAP] > 0)
+        def _():
+            repair(2 * h)
+            repair(2 * h + 1)
+
+        return carry
+
+    lax.fori_loop(0, members // 2, add, 0)
 
     low = low_half(ROWS)
 
@@ -184,8 +212,9 @@
             a = acc_ref[r * members + 2 * g]
             b = acc_ref[r * members + 2 * g + 1]
             lanes = slice(g * LANES, (g + 1) * LANES)
-            op_ref[pl.ds(at, ROWS), lanes] = jnp.where(low, a, turned(b)).astype(jnp.bfloat16)
-            op_ref[pl.ds(at + ROWS, ROWS), lanes] = jnp.where(low, turned(a), b).astype(jnp.bfloat16)
+            swap = turned(jnp.where(low, b, a))
+            op_ref[pl.ds(at, ROWS), lanes] = jnp.where(low, a, swap).astype(jnp.bfloat16)
+            op_ref[pl.ds(at + ROWS, ROWS), lanes] = jnp.where(low, swap, b).astype(jnp.bfloat16)
         return carry
 
     lax.fori_loop(0, kblocks, join, 0)
@@ -213,18 +242,29 @@
             jax.ShapeDtypeStruct(held, f32),
             jax.ShapeDtypeStruct(held, f32),
         ],
-        in_specs=[sspec()] * 4 + [vspec()] * 3,
+        in_specs=[sspec()] * 2 + [vspec()] * 6,
         out_specs=[vspec()] * 3,
         scratch_shapes=[
-            pltpu.SMEM((members,), i32),
-            pltpu.VMEM((members, 1, LANES), i32),
+            pltpu.VMEM((1, tiles), i32),
+            pltpu.SMEM((1, tiles), i32),
+            pltpu.VMEM((members, LANES), f32),
             pltpu.VMEM(held, bf16),
             pltpu.VMEM((kblocks, BLOCK_ROWS + ROWS, LANES), f32),
             rows,
+            pltpu.SemaphoreType.DMA(()),
         ],
         compiler_params=params(16),
         name="fill",
-    )(tile_dest[:, 0], tile_row, tile_col, sel, rates.reshape(tiles, ROWS, LANES), drive, tau)
+    )(
+        tile_dest[:, 0],
+        sel,
+        tile_dest.reshape(1, tiles),
+        tile_row.reshape(1, tiles),
+        tile_col.reshape(1, tiles),
+        rates.reshape(tiles, ROWS, LANES),
+        drive,
+        tau,
+    )
     first = exchange(first)
 
     operator, send = pl.pallas_call(
@@ -237,6 +277,7 @@
         out_specs=[vspec()] * 2,
         scratch_shapes=[
             pltpu.VMEM((kblocks * members + 1, ROWS, LANES), f32),
+            pltpu.VMEM((members, LANES), f32),
             pltpu.VMEM((members, LANES), i32),
             pltpu.SMEM((members, LANES), i32),
             pltpu.VMEM(held, bf16),

time: 210 us -> 209 us (level)
  no operation moved by 1% of the time
where the time goes in v4:
time: 209 us
  blocking collectives  192 us (92%)
  Pallas kernels  14.7 us (7%)
  local copies, waits for them, and re-layouts  2.15 us (1%)
    all_to_all x1, blocking collectives, shards(): first = exchange(first)  101 us
    all_to_all x2, blocking collectives, shards(): exchange(send)  91.2 us
    pallas_call x1, Pallas kernels, shards(): pl.pallas_call(first_kernel, out_shape=[jax.ShapeDtypeStruct((kblocks * H...  7.63 us
    pallas_call x2, Pallas kernels, shards(): pl.pallas_call(functools.partial(step_kernel, last), out_shape=jax.ShapeD...  4.93 us

profile of v4, /device:TPU:1, one launch (start us, length us, event | category | flops | bytes accessed | tf_op | source)
XLA Modules:
  0.0 209.0 jit_solution(7009966480783964805)
XLA Ops:
  0.0 0.0 copy-start.3
  0.0 0.0 copy-start.1
  0.0 0.0 copy-start
  0.0 0.0 copy-start.2
  0.0 0.0 copy-start.5
  0.0 0.0 copy-start.4
  0.0 2.1 %copy.8 = bf16[32,8,32,128]{3,2,1,0:T(8,128)(2,1)S(1)} copy(bf16[32,8,32,128]{3,1,2,0:T(8,128)(2,1)} %bitcast.16) | data formatting | bytes 4194304
  2.2 0.0 copy-done.3
  2.2 0.0 copy-done.1
  2.2 0.0 copy-done
  2.2 0.0 copy-done.2
  2.2 0.0 copy-done.5
  2.2 0.0 copy-done.4
  2.2 2.1 %fill.1 = (bf16[128,232,128]{2,1,0:T(8,128)(2,1)S(1)}, f32[4,96,128]{2,1,0:T(8,128)S(1)}, f32[4,96,128]{2,1,0:T(8,128)S(1)}) custom-call(s32[256]{0:T(256)S(1)} %bitcast.12, s32[128]{0:T(128)S(1)} %bitcast.8, s32[1,256]{1,0:T(1,128)S(1)} %bitcast.13, s32[1,256]{1,0:T(1,128)S(1)} %bitcast.14, s32[1,256]{1,0:T(1,128)S(1)} %bitcast.15, ...), custom_call_target="tpu_custom_call" | custom-call | tf_op jit(solution)/shard_map/fill/pallas_call | solution.py:238
  4.4 100.8 %all_to_all.15.x_ref = bf16[128,232,128]{2,1,0:T(8,128)(2,1)S(1)} all-to-all(bf16[128,232,128]{2,1,0:T(8,128)(2,1)S(1)} %get-tuple-element.10), channel_id=1, replica_groups=mesh['pool'=4,'ka'=32] {'pool','ka'}, dimensions={0} | all-to-all | bytes 15204352 | tf_op jit(solution)/shard_map/all_to_all | solution.py:268
  105.2 7.6 %first.1 = (bf16[256,8192]{1,0:T(8,128)(2,1)S(1)}, bf16[128,96,128]{2,1,0:T(8,128)(2,1)S(1)}) custom-call(s32[128]{0:T(128)S(1)} %bitcast.9, bf16[128,232,128]{2,1,0:T(8,128)(2,1)S(1)} %all_to_all.15.x_ref, f32[4,96,128]{2,1,0:T(8,128)S(1)} %get-tuple-element.11.drive_ref, f32[4,96,128]{2,1,0:T(8,128)S(1)} %get-tuple-element.12.tau_ref), custom_call_target="tpu_custom_call" | custom-call | tf_op jit(solution)/shard_map/first/pallas_call | solution.py:270
  112.8 45.6 %all_to_all.16.x_ref = bf16[128,96,128]{2,1,0:T(8,128)(2,1)S(1)} all-to-all(bf16[128,96,128]{2,1,0:T(8,128)(2,1)S(1)} %get-tuple-element.13), channel_id=1, replica_groups=mesh['pool'=4,'ka'=32] {'pool','ka'}, dimensions={0} | all-to-all | bytes 6291456 | tf_op jit(solution)/shard_map/all_to_all | solution.py:301
  158.4 2.3 %step.1 = bf16[128,96,128]{2,1,0:T(8,128)(2,1)S(1)} custom-call(s32[128]{0:T(128)S(1)} %bitcast.10, bf16[128,96,128]{2,1,0:T(8,128)(2,1)S(1)} %all_to_all.16.x_ref, bf16[256,8192]{1,0:T(8,128)(2,1)S(1)} %get-tuple-element.14.op_ref, f32[4,96,128]{2,1,0:T(8,128)S(1)} %get-tuple-element.11.drive_ref, f32[4,96,128]{2,1,0:T(8,128)S(1)} %get-tuple-element.12.tau_ref), custom_call_target="tpu_custom_call" | custom-call | tf_op jit(solution)/shard_map/step/pallas_call | solution.py:293
  160.7 45.6 %all_to_all.17.x_ref = bf16[128,96,128]{2,1,0:T(8,128)(2,1)S(1)} all-to-all(bf16[128,96,128]{2,1,0:T(8,128)(2,1)S(1)} %step.1), channel_id=1, replica_groups=mesh['pool'=4,'ka'=32] {'pool','ka'}, dimensions={0} | all-to-all | bytes 6291456 | tf_op jit(solution)/shard_map/all_to_all | solution.py:301
  206.3 2.6 %step_last.1 = f32[4,12288]{1,0:T(4,128)} custom-call(s32[128]{0:T(128)S(1)} %bitcast.11, bf16[128,96,128]{2,1,0:T(8,128)(2,1)S(1)} %all_to_all.17.x_ref, bf16[256,8192]{1,0:T(8,128)(2,1)S(1)} %get-tuple-element.14.op_ref, f32[4,96,128]{2,1,0:T(8,128)S(1)} %get-tuple-element.11.drive_ref, f32[4,96,128]{2,1,0:T(8,128)S(1)} %get-tuple-element.12.tau_ref), custom_call_target="tpu_custom_call" | custom-call | tf_op jit(solution)/shard_map/step_last/pallas_call | solution.py:293
Async XLA Ops:
  0.0 2.2 %copy-start.3 = (s32[256,1]{0,1:T(1,128)S(1)}, s32[256,1]{0,1:T(1,128)}, u32[]{:S(2)}) copy-start(s32[256,1]{0,1:T(1,128)} %param.8) | copy-start | bytes 3076
  0.0 2.2 %copy-start.1 = (f32[4,4096]{1,0:T(4,128)S(1)}, f32[4,4096]{1,0:T(4,128)}, u32[]{:S(2)}) copy-start(f32[4,4096]{1,0:T(4,128)} %tau_ref.1) | copy-start | bytes 196612
  0.0 2.2 %copy-start = (f32[4,12288]{1,0:T(4,128)S(1)}, f32[4,12288]{1,0:T(4,128)}, u32[]{:S(2)}) copy-start(f32[4,12288]{1,0:T(4,128)} %drive_ref.1) | copy-start | bytes 589828
  0.0 2.2 %copy-start.2 = (s32[1,128]{1,0:T(1,128)S(1)}, s32[1,128]{1,0:T(1,128)}, u32[]{:S(2)}) copy-start(s32[1,128]{1,0:T(1,128)} %param.11) | copy-start | bytes 1540
  0.0 2.2 %copy-start.5 = (s32[256]{0:T(256)S(1)}, s32[256]{0:T(256)}, u32[]{:S(2)}) copy-start(s32[256]{0:T(256)} %param.10) | copy-start | bytes 3076
  0.0 2.2 %copy-start.4 = (s32[256]{0:T(256)S(1)}, s32[256]{0:T(256)}, u32[]{:S(2)}) copy-start(s32[256]{0:T(256)} %param.9) | copy-start | bytes 3076

commit v5 on v4

--- a/solution.py
+++ b/solution.py
@@ -112,16 +112,24 @@
     lax.fori_loop(0, tiles, move, 0, unroll=8)
 
 
-def advance(last, op_ref, x_ref, x_at, sel_ref, drive_ref, tau_ref, out_ref, new_ref, rows_ref):
+def advance(last, op_ref, x_ref, x_at, sel_ref, drive_ref, tau_ref, out_ref, new_ref, rows_ref, prepare=None, chunks=1):
     members = x_ref.shape[0]
     kblocks = drive_ref.shape[0]
     low = low_half(ROWS)
     zero = jnp.zeros((), jnp.bfloat16)
-    third = x_ref[:, x_at + HALF : x_at + BLOCK_ROWS, :]
-    third = jnp.concatenate([jnp.where(low, third, zero), jnp.where(low, zero, third)], axis=1)
-    pair = x_ref[:, x_at : x_at + HALF, :]
-    right = jnp.concatenate([v.reshape(members * HALF, LANES) for v in (pair, third)], axis=1)
-    total = jnp.dot(op_ref[...], right, preferred_element_type=jnp.float32)
+    some = members // chunks
+    total = None
+    for q in range(chunks):
+        if prepare is not None:
+            prepare(q)
+        entries = slice(q * some, (q + 1) * some)
+        third = x_ref[entries, x_at + HALF : x_at + BLOCK_ROWS, :]
+        third = jnp.concatenate([jnp.where(low, third, zero), jnp.where(low, zero, third)], axis=1)
+        pair = x_ref[entries, x_at : x_at + HALF, :]
+        right = jnp.concatenate([v.reshape(some * HALF, LANES) for v in (pair, third)], axis=1)
+        left = op_ref[:, q * some * HALF : (q + 1) * some * HALF]
+        part = jnp.dot(left, right, preferred_element_type=jnp.float32)
+        total = part if total is None else total + part
     for r in range(kblocks):
         at = r * HALF
         pair = drive_ref[r, : 2 * ROWS, :] + tau_ref[r, : 2 * ROWS, :] * total[at : at + HALF, :LANES]
@@ -162,63 +170,44 @@
     lax.fori_loop(0, members, read, 0, unroll=8)
     raw = raw_ref[...]
     place = (raw * 8.0 + pltpu.roll(raw, LANES - CAP, 1)).astype(jnp.int32) + none
-    lane = lax.broadcasted_iota(jnp.int32, place.shape, 1)
-    lost = jnp.zeros_like(place)
-    for k in range(1, CAP):
-        again = (place == pltpu.roll(place, LANES - k, 1)) & (lane < CAP - k) & (place < none)
-        lost = jnp.where(again, 1, lost)
-    some = lost
-    for k in range(1, CAP):
-        some = some + pltpu.roll(lost, k, 1)
-    place = jnp.where(lane < CAP, place, jnp.where(lane < 2 * CAP, pltpu.roll(lost, CAP, 1), pltpu.roll(some, CAP + 1, 1)))
     lab_ref[...] = place
     copy = pltpu.make_async_copy(lab_ref, at_ref, sem)
     copy.start()
     acc_ref[...] = jnp.zeros_like(acc_ref)
     copy.wait()
 
-    def tile(s, c):
-        return x_ref[s, c * ROWS : (c + 1) * ROWS, :].astype(jnp.float32)
-
-    def repair(s):
-        for c in range(CAP - 1):
-
-            @pl.when(at_ref[s, CAP + c] > 0)
-            def _():
-                at = at_ref[s, c]
-                acc_ref[at] = acc_ref[at] + tile(s, c)
-
-    def add(h, carry):
-        for s in (2 * h, 2 * h + 1):
-            ats = [at_ref[s, c] for c in range(CAP)]
-            news = [acc_ref[ats[c]] + tile(s, c) for c in range(CAP)]
-            for c in range(CAP):
-                acc_ref[ats[c]] = news[c]
-
-        @pl.when(at_ref[2 * h, 2 * CAP] + at_ref[2 * h + 1, 2 * CAP] > 0)
-        def _():
-            repair(2 * h)
-            repair(2 * h + 1)
-
-        return carry
-
-    lax.fori_loop(0, members // 2, add, 0)
-
-    low = low_half(ROWS)
-
-    def join(r, carry):
-        at = pl.multiple_of(r * HALF, HALF)
-        for g in range(members // 2):
-            a = acc_ref[r * members + 2 * g]
-            b = acc_ref[r * members + 2 * g + 1]
-            lanes = slice(g * LANES, (g + 1) * LANES)
-            swap = turned(jnp.where(low, b, a))
-            op_ref[pl.ds(at, ROWS), lanes] = jnp.where(low, a, swap).astype(jnp.bfloat16)
-            op_ref[pl.ds(at + ROWS, ROWS), lanes] = jnp.where(low, swap, b).astype(jnp.bfloat16)
-        return carry
-
-    lax.fori_loop(0, kblocks, join, 0)
-    advance(False, op_ref, x_ref, TILE_ROWS, sel_ref, drive_ref, tau_ref, out_ref, pk_ref, rows_ref)
+    def add(s, carry):
+        ats = [at_ref[s, c] for c in range(CAP)]
+        olds = [acc_ref[at] for at in ats]
+        sums = []
+        for c in range(CAP):
+            same = jnp.zeros((ROWS, LANES), jnp.float32)
+            for e in range(c):
+                same = jnp.where(ats[e] == ats[c], sums[e], same)
+            tile = x_ref[s, c * ROWS : (c + 1) * ROWS, :].astype(jnp.float32)
+            sums.append(tile + same if c else tile)
+        for c in range(CAP):
+            acc_ref[ats[c]] = olds[c] + sums[c]
+        return carry
+
+    lax.fori_loop(0, members, add, 0, unroll=4)
+
+    low = low_half(ROWS)
+
+    pairs = members // 2 // 16
+
+    def join(q):
+        for g in range(q * pairs, (q + 1) * pairs):
+            for r in range(kblocks):
+                at = r * HALF
+                a = acc_ref[r * members + 2 * g]
+                b = acc_ref[r * members + 2 * g + 1]
+                lanes = slice(g * LANES, (g + 1) * LANES)
+                swap = turned(jnp.where(low, b, a))
+                op_ref[at : at + ROWS, lanes] = jnp.where(low, a, swap).astype(jnp.bfloat16)
+                op_ref[at + ROWS : at + HALF, lanes] = jnp.where(low, swap, b).astype(jnp.bfloat16)
+
+    advance(False, op_ref, x_ref, TILE_ROWS, sel_ref, drive_ref, tau_ref, out_ref, pk_ref, rows_ref, join, 16)
 
 
 def step_kernel(last, sel_ref, x_ref, op_ref, drive_ref, tau_ref, out_ref, new_ref, rows_ref):

time: 209 us -> 209 us (level)
  no operation moved by 1% of the time
where the time goes in v5:
time: 209 us; the launch traced here: 208 us
  blocking collectives  192 us (92%)
  Pallas kernels  14.1 us (7%)
  local copies, waits for them, and re-layouts  2.15 us (1%)
    all_to_all x1, blocking collectives, shards(): first = exchange(first)  101 us
    all_to_all x2, blocking collectives, shards(): exchange(send)  91.2 us
    pallas_call x1, Pallas kernels, shards(): pl.pallas_call(first_kernel, out_shape=[jax.ShapeDtypeStruct((kblocks * H...  7.05 us
    pallas_call x2, Pallas kernels, shards(): pl.pallas_call(functools.partial(step_kernel, last), out_shape=jax.ShapeD...  4.93 us

profile of v5, /device:TPU:1, one launch (start us, length us, event | category | flops | bytes accessed | tf_op | source)
XLA Modules:
  0.0 208.4 jit_solution(17853586593568471653)
XLA Ops:
  0.0 0.0 copy-start.3
  0.0 0.0 copy-start.1
  0.0 0.0 copy-start
  0.0 0.0 copy-start.2
  0.0 0.0 copy-start.5
  0.0 0.0 copy-start.4
  0.0 2.1 %copy.8 = bf16[32,8,32,128]{3,2,1,0:T(8,128)(2,1)S(1)} copy(bf16[32,8,32,128]{3,1,2,0:T(8,128)(2,1)} %bitcast.16) | data formatting | bytes 4194304
  2.2 0.0 copy-done.3
  2.2 0.0 copy-done.1
  2.2 0.0 copy-done
  2.2 0.0 copy-done.2
  2.2 0.0 copy-done.5
  2.2 0.0 copy-done.4
  2.2 2.1 %fill.1 = (bf16[128,232,128]{2,1,0:T(8,128)(2,1)S(1)}, f32[4,96,128]{2,1,0:T(8,128)S(1)}, f32[4,96,128]{2,1,0:T(8,128)S(1)}) custom-call(s32[256]{0:T(256)S(1)} %bitcast.12, s32[128]{0:T(128)S(1)} %bitcast.8, s32[1,256]{1,0:T(1,128)S(1)} %bitcast.13, s32[1,256]{1,0:T(1,128)S(1)} %bitcast.14, s32[1,256]{1,0:T(1,128)S(1)} %bitcast.15, ...), custom_call_target="tpu_custom_call" | custom-call | tf_op jit(solution)/shard_map/fill/pallas_call | solution.py:227
  4.4 100.8 %all_to_all.15.x_ref = bf16[128,232,128]{2,1,0:T(8,128)(2,1)S(1)} all-to-all(bf16[128,232,128]{2,1,0:T(8,128)(2,1)S(1)} %get-tuple-element.10), channel_id=1, replica_groups=mesh['pool'=4,'ka'=32] {'pool','ka'}, dimensions={0} | all-to-all | bytes 15204352 | tf_op jit(solution)/shard_map/all_to_all | solution.py:257
  105.2 7.1 %first.1 = (bf16[256,8192]{1,0:T(8,128)(2,1)S(1)}, bf16[128,96,128]{2,1,0:T(8,128)(2,1)S(1)}) custom-call(s32[128]{0:T(128)S(1)} %bitcast.9, bf16[128,232,128]{2,1,0:T(8,128)(2,1)S(1)} %all_to_all.15.x_ref, f32[4,96,128]{2,1,0:T(8,128)S(1)} %get-tuple-element.11.drive_ref, f32[4,96,128]{2,1,0:T(8,128)S(1)} %get-tuple-element.12.tau_ref), custom_call_target="tpu_custom_call" | custom-call | tf_op jit(solution)/shard_map/first/pallas_call | solution.py:259
  112.3 45.6 %all_to_all.16.x_ref = bf16[128,96,128]{2,1,0:T(8,128)(2,1)S(1)} all-to-all(bf16[128,96,128]{2,1,0:T(8,128)(2,1)S(1)} %get-tuple-element.13), channel_id=1, replica_groups=mesh['pool'=4,'ka'=32] {'pool','ka'}, dimensions={0} | all-to-all | bytes 6291456 | tf_op jit(solution)/shard_map/all_to_all | solution.py:290
  157.8 2.3 %step.1 = bf16[128,96,128]{2,1,0:T(8,128)(2,1)S(1)} custom-call(s32[128]{0:T(128)S(1)} %bitcast.10, bf16[128,96,128]{2,1,0:T(8,128)(2,1)S(1)} %all_to_all.16.x_ref, bf16[256,8192]{1,0:T(8,128)(2,1)S(1)} %get-tuple-element.14.op_ref, f32[4,96,128]{2,1,0:T(8,128)S(1)} %get-tuple-element.11.drive_ref, f32[4,96,128]{2,1,0:T(8,128)S(1)} %get-tuple-element.12.tau_ref), custom_call_target="tpu_custom_call" | custom-call | tf_op jit(solution)/shard_map/step/pallas_call | solution.py:282
  160.1 45.6 %all_to_all.17.x_ref = bf16[128,96,128]{2,1,0:T(8,128)(2,1)S(1)} all-to-all(bf16[128,96,128]{2,1,0:T(8,128)(2,1)S(1)} %step.1), channel_id=1, replica_groups=mesh['pool'=4,'ka'=32] {'pool','ka'}, dimensions={0} | all-to-all | bytes 6291456 | tf_op jit(solution)/shard_map/all_to_all | solution.py:290
  205.7 2.6 %step_last.1 = f32[4,12288]{1,0:T(4,128)} custom-call(s32[128]{0:T(128)S(1)} %bitcast.11, bf16[128,96,128]{2,1,0:T(8,128)(2,1)S(1)} %all_to_all.17.x_ref, bf16[256,8192]{1,0:T(8,128)(2,1)S(1)} %get-tuple-element.14.op_ref, f32[4,96,128]{2,1,0:T(8,128)S(1)} %get-tuple-element.11.drive_ref, f32[4,96,128]{2,1,0:T(8,128)S(1)} %get-tuple-element.12.tau_ref), custom_call_target="tpu_custom_call" | custom-call | tf_op jit(solution)/shard_map/step_last/pallas_call | solution.py:282
Async XLA Ops:
  0.0 2.2 %copy-start.3 = (s32[256,1]{0,1:T(1,128)S(1)}, s32[256,1]{0,1:T(1,128)}, u32[]{:S(2)}) copy-start(s32[256,1]{0,1:T(1,128)} %param.8) | copy-start | bytes 3076
  0.0 2.2 %copy-start.1 = (f32[4,4096]{1,0:T(4,128)S(1)}, f32[4,4096]{1,0:T(4,128)}, u32[]{:S(2)}) copy-start(f32[4,4096]{1,0:T(4,128)} %tau_ref.1) | copy-start | bytes 196612
  0.0 2.2 %copy-start = (f32[4,12288]{1,0:T(4,128)S(1)}, f32[4,12288]{1,0:T(4,128)}, u32[]{:S(2)}) copy-start(f32[4,12288]{1,0:T(4,128)} %drive_ref.1) | copy-start | bytes 589828
  0.0 2.2 %copy-start.2 = (s32[1,128]{1,0:T(1,128)S(1)}, s32[1,128]{1,0:T(1,128)}, u32[]{:S(2)}) copy-start(s32[1,128]{1,0:T(1,128)} %param.11) | copy-start | bytes 1540
  0.0 2.2 %copy-start.5 = (s32[256]{0:T(256)S(1)}, s32[256]{0:T(256)}, u32[]{:S(2)}) copy-start(s32[256]{0:T(256)} %param.10) | copy-start | bytes 3076
  0.0 2.2 %copy-start.4 = (s32[256]{0:T(256)S(1)}, s32[256]{0:T(256)}, u32[]{:S(2)}) copy-start(s32[256]{0:T(256)} %param.9) | copy-start | bytes 3076

commit v6 on v5

--- a/solution.py
+++ b/solution.py
@@ -200,18 +200,18 @@
         for g in range(q * pairs, (q + 1) * pairs):
             for r in range(kblocks):
                 at = r * HALF
-                a = acc_ref[r * members + 2 * g]
-                b = acc_ref[r * members + 2 * g + 1]
+                a = acc_ref[r * members + 2 * g].astype(jnp.bfloat16)
+                b = acc_ref[r * members + 2 * g + 1].astype(jnp.bfloat16)
                 lanes = slice(g * LANES, (g + 1) * LANES)
                 swap = turned(jnp.where(low, b, a))
-                op_ref[at : at + ROWS, lanes] = jnp.where(low, a, swap).astype(jnp.bfloat16)
-                op_ref[at + ROWS : at + HALF, lanes] = jnp.where(low, swap, b).astype(jnp.bfloat16)
+                op_ref[at : at + ROWS, lanes] = jnp.where(low, a, swap)
+                op_ref[at + ROWS : at + HALF, lanes] = jnp.where(low, swap, b)
 
     advance(False, op_ref, x_ref, TILE_ROWS, sel_ref, drive_ref, tau_ref, out_ref, pk_ref, rows_ref, join, 16)
 
 
 def step_kernel(last, sel_ref, x_ref, op_ref, drive_ref, tau_ref, out_ref, new_ref, rows_ref):
-    advance(last, op_ref, x_ref, 0, sel_ref, drive_ref, tau_ref, out_ref, new_ref, rows_ref)
+    advance(last, op_ref, x_ref, 0, sel_ref, drive_ref, tau_ref, out_ref, new_ref, rows_ref, None, 16)
 
 
 def shards(rates, tile_dest, tile_row, tile_col, send_list, drive, tau):

time: 209 us -> 208 us (level)
  no operation moved by 1% of the time
where the time goes in v6:
time: 208 us
  blocking collectives  192 us (92%)
  Pallas kernels  13.8 us (7%)
  local copies, waits for them, and re-layouts  2.15 us (1%)
    all_to_all x1, blocking collectives, shards(): first = exchange(first)  101 us
    all_to_all x2, blocking collectives, shards(): exchange(send)  91.3 us
    pallas_call x1, Pallas kernels, shards(): pl.pallas_call(first_kernel, out_shape=[jax.ShapeDtypeStruct((kblocks * H...  6.72 us
    pallas_call x2, Pallas kernels, shards(): pl.pallas_call(functools.partial(step_kernel, last), out_shape=jax.ShapeD...  4.93 us

profile of v6, /device:TPU:1, one launch (start us, length us, event | category | flops | bytes accessed | tf_op | source)
XLA Modules:
  0.0 208.1 jit_solution(10226882227663242122)
XLA Ops:
  0.0 0.0 copy-start.3
  0.0 0.0 copy-start.1
  0.0 0.0 copy-start
  0.0 0.0 copy-start.2
  0.0 0.0 copy-start.5
  0.0 0.0 copy-start.4
  0.0 2.1 %copy.8 = bf16[32,8,32,128]{3,2,1,0:T(8,128)(2,1)S(1)} copy(bf16[32,8,32,128]{3,1,2,0:T(8,128)(2,1)} %bitcast.16) | data formatting | bytes 4194304
  2.2 0.0 copy-done.3
  2.2 0.0 copy-done.1
  2.2 0.0 copy-done
  2.2 0.0 copy-done.2
  2.2 0.0 copy-done.5
  2.2 0.0 copy-done.4
  2.2 2.1 %fill.1 = (bf16[128,232,128]{2,1,0:T(8,128)(2,1)S(1)}, f32[4,96,128]{2,1,0:T(8,128)S(1)}, f32[4,96,128]{2,1,0:T(8,128)S(1)}) custom-call(s32[256]{0:T(256)S(1)} %bitcast.12, s32[128]{0:T(128)S(1)} %bitcast.8, s32[1,256]{1,0:T(1,128)S(1)} %bitcast.13, s32[1,256]{1,0:T(1,128)S(1)} %bitcast.14, s32[1,256]{1,0:T(1,128)S(1)} %bitcast.15, ...), custom_call_target="tpu_custom_call" | custom-call | tf_op jit(solution)/shard_map/fill/pallas_call | solution.py:227
  4.4 100.8 %all_to_all.15.x_ref = bf16[128,232,128]{2,1,0:T(8,128)(2,1)S(1)} all-to-all(bf16[128,232,128]{2,1,0:T(8,128)(2,1)S(1)} %get-tuple-element.10), channel_id=1, replica_groups=mesh['pool'=4,'ka'=32] {'pool','ka'}, dimensions={0} | all-to-all | bytes 15204352 | tf_op jit(solution)/shard_map/all_to_all | solution.py:257
  105.2 6.7 %first.1 = (bf16[256,8192]{1,0:T(8,128)(2,1)S(1)}, bf16[128,96,128]{2,1,0:T(8,128)(2,1)S(1)}) custom-call(s32[128]{0:T(128)S(1)} %bitcast.9, bf16[128,232,128]{2,1,0:T(8,128)(2,1)S(1)} %all_to_all.15.x_ref, f32[4,96,128]{2,1,0:T(8,128)S(1)} %get-tuple-element.11.drive_ref, f32[4,96,128]{2,1,0:T(8,128)S(1)} %get-tuple-element.12.tau_ref), custom_call_target="tpu_custom_call" | custom-call | tf_op jit(solution)/shard_map/first/pallas_call | solution.py:259
  111.9 45.6 %all_to_all.16.x_ref = bf16[128,96,128]{2,1,0:T(8,128)(2,1)S(1)} all-to-all(bf16[128,96,128]{2,1,0:T(8,128)(2,1)S(1)} %get-tuple-element.13), channel_id=1, replica_groups=mesh['pool'=4,'ka'=32] {'pool','ka'}, dimensions={0} | all-to-all | bytes 6291456 | tf_op jit(solution)/shard_map/all_to_all | solution.py:290
  157.5 2.3 %step.1 = bf16[128,96,128]{2,1,0:T(8,128)(2,1)S(1)} custom-call(s32[128]{0:T(128)S(1)} %bitcast.10, bf16[128,96,128]{2,1,0:T(8,128)(2,1)S(1)} %all_to_all.16.x_ref, bf16[256,8192]{1,0:T(8,128)(2,1)S(1)} %get-tuple-element.14.op_ref, f32[4,96,128]{2,1,0:T(8,128)S(1)} %get-tuple-element.11.drive_ref, f32[4,96,128]{2,1,0:T(8,128)S(1)} %get-tuple-element.12.tau_ref), custom_call_target="tpu_custom_call" | custom-call | tf_op jit(solution)/shard_map/step/pallas_call | solution.py:282
  159.9 45.6 %all_to_all.17.x_ref = bf16[128,96,128]{2,1,0:T(8,128)(2,1)S(1)} all-to-all(bf16[128,96,128]{2,1,0:T(8,128)(2,1)S(1)} %step.1), channel_id=1, replica_groups=mesh['pool'=4,'ka'=32] {'pool','ka'}, dimensions={0} | all-to-all | bytes 6291456 | tf_op jit(solution)/shard_map/all_to_all | solution.py:290
  205.5 2.6 %step_last.1 = f32[4,12288]{1,0:T(4,128)} custom-call(s32[128]{0:T(128)S(1)} %bitcast.11, bf16[128,96,128]{2,1,0:T(8,128)(2,1)S(1)} %all_to_all.17.x_ref, bf16[256,8192]{1,0:T(8,128)(2,1)S(1)} %get-tuple-element.14.op_ref, f32[4,96,128]{2,1,0:T(8,128)S(1)} %get-tuple-element.11.drive_ref, f32[4,96,128]{2,1,0:T(8,128)S(1)} %get-tuple-element.12.tau_ref), custom_call_target="tpu_custom_call" | custom-call | tf_op jit(solution)/shard_map/step_last/pallas_call | solution.py:282
Async XLA Ops:
  0.0 2.2 %copy-start.3 = (s32[256,1]{0,1:T(1,128)S(1)}, s32[256,1]{0,1:T(1,128)}, u32[]{:S(2)}) copy-start(s32[256,1]{0,1:T(1,128)} %param.8) | copy-start | bytes 3076
  0.0 2.2 %copy-start.1 = (f32[4,4096]{1,0:T(4,128)S(1)}, f32[4,4096]{1,0:T(4,128)}, u32[]{:S(2)}) copy-start(f32[4,4096]{1,0:T(4,128)} %tau_ref.1) | copy-start | bytes 196612
  0.0 2.2 %copy-start = (f32[4,12288]{1,0:T(4,128)S(1)}, f32[4,12288]{1,0:T(4,128)}, u32[]{:S(2)}) copy-start(f32[4,12288]{1,0:T(4,128)} %drive_ref.1) | copy-start | bytes 589828
  0.0 2.2 %copy-start.2 = (s32[1,128]{1,0:T(1,128)S(1)}, s32[1,128]{1,0:T(1,128)}, u32[]{:S(2)}) copy-start(s32[1,128]{1,0:T(1,128)} %param.11) | copy-start | bytes 1540
  0.0 2.2 %copy-start.5 = (s32[256]{0:T(256)S(1)}, s32[256]{0:T(256)}, u32[]{:S(2)}) copy-start(s32[256]{0:T(256)} %param.10) | copy-start | bytes 3076
  0.0 2.2 %copy-start.4 = (s32[256]{0:T(256)S(1)}, s32[256]{0:T(256)}, u32[]{:S(2)}) copy-start(s32[256]{0:T(256)} %param.9) | copy-start | bytes 3076

commit v7 on v6

--- a/solution.py
+++ b/solution.py
@@ -109,7 +109,7 @@
         out_ref[dest_ref[i], pl.ds(start, ROWS), :] = rates_ref[i]
         return carry
 
-    lax.fori_loop(0, tiles, move, 0, unroll=8)
+    lax.fori_loop(0, tiles, move, 0, unroll=16)
 
 
 def advance(last, op_ref, x_ref, x_at, sel_ref, drive_ref, tau_ref, out_ref, new_ref, rows_ref, prepare=None, chunks=1):
@@ -190,7 +190,7 @@
             acc_ref[ats[c]] = olds[c] + sums[c]
         return carry
 
-    lax.fori_loop(0, members, add, 0, unroll=4)
+    lax.fori_loop(0, members, add, 0, unroll=8)
 
     low = low_half(ROWS)
 

time: 208 us -> 208 us (level)
  no operation moved by 1% of the time
where the time goes in v7:
time: 208 us
  blocking collectives  192 us (92%)
  Pallas kernels  13.7 us (7%)
  local copies, waits for them, and re-layouts  2.15 us (1%)
    all_to_all x1, blocking collectives, shards(): first = exchange(first)  101 us
    all_to_all x2, blocking collectives, shards(): exchange(send)  91.2 us
    pallas_call x1, Pallas kernels, shards(): pl.pallas_call(first_kernel, out_shape=[jax.ShapeDtypeStruct((kblocks * H...  6.68 us
    pallas_call x2, Pallas kernels, shards(): pl.pallas_call(functools.partial(step_kernel, last), out_shape=jax.ShapeD...  4.93 us

profile of v7, /device:TPU:1, one launch (start us, length us, event | category | flops | bytes accessed | tf_op | source)
XLA Modules:
  0.0 207.9 jit_solution(2077928748096765290)
XLA Ops:
  0.0 0.0 copy-start.3
  0.0 0.0 copy-start.1
  0.0 0.0 copy-start
  0.0 0.0 copy-start.2
  0.0 0.0 copy-start.5
  0.0 0.0 copy-start.4
  0.0 2.1 %copy.8 = bf16[32,8,32,128]{3,2,1,0:T(8,128)(2,1)S(1)} copy(bf16[32,8,32,128]{3,1,2,0:T(8,128)(2,1)} %bitcast.16) | data formatting | bytes 4194304
  2.2 0.0 copy-done.3
  2.2 0.0 copy-done.1
  2.2 0.0 copy-done
  2.2 0.0 copy-done.2
  2.2 0.0 copy-done.5
  2.2 0.0 copy-done.4
  2.2 2.1 %fill.1 = (bf16[128,232,128]{2,1,0:T(8,128)(2,1)S(1)}, f32[4,96,128]{2,1,0:T(8,128)S(1)}, f32[4,96,128]{2,1,0:T(8,128)S(1)}) custom-call(s32[256]{0:T(256)S(1)} %bitcast.12, s32[128]{0:T(128)S(1)} %bitcast.8, s32[1,256]{1,0:T(1,128)S(1)} %bitcast.13, s32[1,256]{1,0:T(1,128)S(1)} %bitcast.14, s32[1,256]{1,0:T(1,128)S(1)} %bitcast.15, ...), custom_call_target="tpu_custom_call" | custom-call | tf_op jit(solution)/shard_map/fill/pallas_call | solution.py:227
  4.3 100.8 %all_to_all.15.x_ref = bf16[128,232,128]{2,1,0:T(8,128)(2,1)S(1)} all-to-all(bf16[128,232,128]{2,1,0:T(8,128)(2,1)S(1)} %get-tuple-element.10), channel_id=1, replica_groups=mesh['pool'=4,'ka'=32] {'pool','ka'}, dimensions={0} | all-to-all | bytes 15204352 | tf_op jit(solution)/shard_map/all_to_all | solution.py:257
  105.1 6.7 %first.1 = (bf16[256,8192]{1,0:T(8,128)(2,1)S(1)}, bf16[128,96,128]{2,1,0:T(8,128)(2,1)S(1)}) custom-call(s32[128]{0:T(128)S(1)} %bitcast.9, bf16[128,232,128]{2,1,0:T(8,128)(2,1)S(1)} %all_to_all.15.x_ref, f32[4,96,128]{2,1,0:T(8,128)S(1)} %get-tuple-element.11.drive_ref, f32[4,96,128]{2,1,0:T(8,128)S(1)} %get-tuple-element.12.tau_ref), custom_call_target="tpu_custom_call" | custom-call | tf_op jit(solution)/shard_map/first/pallas_call | solution.py:259
  111.8 45.5 %all_to_all.16.x_ref = bf16[128,96,128]{2,1,0:T(8,128)(2,1)S(1)} all-to-all(bf16[128,96,128]{2,1,0:T(8,128)(2,1)S(1)} %get-tuple-element.13), channel_id=1, replica_groups=mesh['pool'=4,'ka'=32] {'pool','ka'}, dimensions={0} | all-to-all | bytes 6291456 | tf_op jit(solution)/shard_map/all_to_all | solution.py:290
  157.3 2.3 %step.1 = bf16[128,96,128]{2,1,0:T(8,128)(2,1)S(1)} custom-call(s32[128]{0:T(128)S(1)} %bitcast.10, bf16[128,96,128]{2,1,0:T(8,128)(2,1)S(1)} %all_to_all.16.x_ref, bf16[256,8192]{1,0:T(8,128)(2,1)S(1)} %get-tuple-element.14.op_ref, f32[4,96,128]{2,1,0:T(8,128)S(1)} %get-tuple-element.11.drive_ref, f32[4,96,128]{2,1,0:T(8,128)S(1)} %get-tuple-element.12.tau_ref), custom_call_target="tpu_custom_call" | custom-call | tf_op jit(solution)/shard_map/step/pallas_call | solution.py:282
  159.6 45.6 %all_to_all.17.x_ref = bf16[128,96,128]{2,1,0:T(8,128)(2,1)S(1)} all-to-all(bf16[128,96,128]{2,1,0:T(8,128)(2,1)S(1)} %step.1), channel_id=1, replica_groups=mesh['pool'=4,'ka'=32] {'pool','ka'}, dimensions={0} | all-to-all | bytes 6291456 | tf_op jit(solution)/shard_map/all_to_all | solution.py:290
  205.3 2.6 %step_last.1 = f32[4,12288]{1,0:T(4,128)} custom-call(s32[128]{0:T(128)S(1)} %bitcast.11, bf16[128,96,128]{2,1,0:T(8,128)(2,1)S(1)} %all_to_all.17.x_ref, bf16[256,8192]{1,0:T(8,128)(2,1)S(1)} %get-tuple-element.14.op_ref, f32[4,96,128]{2,1,0:T(8,128)S(1)} %get-tuple-element.11.drive_ref, f32[4,96,128]{2,1,0:T(8,128)S(1)} %get-tuple-element.12.tau_ref), custom_call_target="tpu_custom_call" | custom-call | tf_op jit(solution)/shard_map/step_last/pallas_call | solution.py:282
Async XLA Ops:
  0.0 2.2 %copy-start.3 = (s32[256,1]{0,1:T(1,128)S(1)}, s32[256,1]{0,1:T(1,128)}, u32[]{:S(2)}) copy-start(s32[256,1]{0,1:T(1,128)} %param.8) | copy-start | bytes 3076
  0.0 2.2 %copy-start.1 = (f32[4,4096]{1,0:T(4,128)S(1)}, f32[4,4096]{1,0:T(4,128)}, u32[]{:S(2)}) copy-start(f32[4,4096]{1,0:T(4,128)} %tau_ref.1) | copy-start | bytes 196612
  0.0 2.2 %copy-start = (f32[4,12288]{1,0:T(4,128)S(1)}, f32[4,12288]{1,0:T(4,128)}, u32[]{:S(2)}) copy-start(f32[4,12288]{1,0:T(4,128)} %drive_ref.1) | copy-start | bytes 589828
  0.0 2.2 %copy-start.2 = (s32[1,128]{1,0:T(1,128)S(1)}, s32[1,128]{1,0:T(1,128)}, u32[]{:S(2)}) copy-start(s32[1,128]{1,0:T(1,128)} %param.11) | copy-start | bytes 1540
  0.0 2.2 %copy-start.5 = (s32[256]{0:T(256)S(1)}, s32[256]{0:T(256)}, u32[]{:S(2)}) copy-start(s32[256]{0:T(256)} %param.10) | copy-start | bytes 3076
  0.0 2.2 %copy-start.4 = (s32[256]{0:T(256)S(1)}, s32[256]{0:T(256)}, u32[]{:S(2)}) copy-start(s32[256]{0:T(256)} %param.9) | copy-start | bytes 3076

commit v8 on v7

--- a/solution.py
+++ b/solution.py
@@ -101,7 +101,7 @@
         out_ref[d, LABEL_AT:FIRST_ROWS, :] = jnp.broadcast_to(lab_ref[pl.ds(d, 1), :], (8, LANES)).astype(bf16)
         return carry
 
-    lax.fori_loop(0, members, block, 0, unroll=8)
+    lax.fori_loop(0, members, block, 0, unroll=16)
     copy.wait()
 
     def move(i, carry):
@@ -154,7 +154,7 @@
             out_ref[d] = new_ref[sel_ref[d]]
             return carry
 
-        lax.fori_loop(0, members, block, 0, unroll=8)
+        lax.fori_loop(0, members, block, 0, unroll=16)
 
 
 def first_kernel(sel_ref, x_ref, drive_ref, tau_ref, op_ref, out_ref, acc_ref, raw_ref, lab_ref, at_ref, pk_ref, rows_ref, sem):
@@ -190,7 +190,7 @@
             acc_ref[ats[c]] = olds[c] + sums[c]
         return carry
 
-    lax.fori_loop(0, members, add, 0, unroll=8)
+    lax.fori_loop(0, members, add, 0, unroll=16)
 
     low = low_half(ROWS)
 

time: 208 us -> 208 us (level)
  no operation moved by 1% of the time
where the time goes in v8:
time: 208 us
  blocking collectives  192 us (92%)
  Pallas kernels  13.5 us (6%)
  local copies, waits for them, and re-layouts  2.15 us (1%)
    all_to_all x1, blocking collectives, shards(): first = exchange(first)  101 us
    all_to_all x2, blocking collectives, shards(): exchange(send)  91.2 us
    pallas_call x1, Pallas kernels, shards(): pl.pallas_call(first_kernel, out_shape=[jax.ShapeDtypeStruct((kblocks * H...  6.52 us
    pallas_call x2, Pallas kernels, shards(): pl.pallas_call(functools.partial(step_kernel, last), out_shape=jax.ShapeD...  4.89 us

profile of v8, /device:TPU:1, one launch (start us, length us, event | category | flops | bytes accessed | tf_op | source)
XLA Modules:
  0.0 207.7 jit_solution(4879596183369181959)
XLA Ops:
  0.0 0.0 copy-start.3
  0.0 0.0 copy-start.1
  0.0 0.0 copy-start
  0.0 0.0 copy-start.2
  0.0 0.0 copy-start.5
  0.0 0.0 copy-start.4
  0.0 2.1 %copy.8 = bf16[32,8,32,128]{3,2,1,0:T(8,128)(2,1)S(1)} copy(bf16[32,8,32,128]{3,1,2,0:T(8,128)(2,1)} %bitcast.16) | data formatting | bytes 4194304
  2.2 0.0 copy-done.3
  2.2 0.0 copy-done.1
  2.2 0.0 copy-done
  2.2 0.0 copy-done.2
  2.2 0.0 copy-done.5
  2.2 0.0 copy-done.4
  2.2 2.1 %fill.1 = (bf16[128,232,128]{2,1,0:T(8,128)(2,1)S(1)}, f32[4,96,128]{2,1,0:T(8,128)S(1)}, f32[4,96,128]{2,1,0:T(8,128)S(1)}) custom-call(s32[256]{0:T(256)S(1)} %bitcast.12, s32[128]{0:T(128)S(1)} %bitcast.8, s32[1,256]{1,0:T(1,128)S(1)} %bitcast.13, s32[1,256]{1,0:T(1,128)S(1)} %bitcast.14, s32[1,256]{1,0:T(1,128)S(1)} %bitcast.15, ...), custom_call_target="tpu_custom_call" | custom-call | tf_op jit(solution)/shard_map/fill/pallas_call | solution.py:227
  4.3 100.8 %all_to_all.15.x_ref = bf16[128,232,128]{2,1,0:T(8,128)(2,1)S(1)} all-to-all(bf16[128,232,128]{2,1,0:T(8,128)(2,1)S(1)} %get-tuple-element.10), channel_id=1, replica_groups=mesh['pool'=4,'ka'=32] {'pool','ka'}, dimensions={0} | all-to-all | bytes 15204352 | tf_op jit(solution)/shard_map/all_to_all | solution.py:257
  105.1 6.5 %first.1 = (bf16[256,8192]{1,0:T(8,128)(2,1)S(1)}, bf16[128,96,128]{2,1,0:T(8,128)(2,1)S(1)}) custom-call(s32[128]{0:T(128)S(1)} %bitcast.9, bf16[128,232,128]{2,1,0:T(8,128)(2,1)S(1)} %all_to_all.15.x_ref, f32[4,96,128]{2,1,0:T(8,128)S(1)} %get-tuple-element.11.drive_ref, f32[4,96,128]{2,1,0:T(8,128)S(1)} %get-tuple-element.12.tau_ref), custom_call_target="tpu_custom_call" | custom-call | tf_op jit(solution)/shard_map/first/pallas_call | solution.py:259
  111.7 45.6 %all_to_all.16.x_ref = bf16[128,96,128]{2,1,0:T(8,128)(2,1)S(1)} all-to-all(bf16[128,96,128]{2,1,0:T(8,128)(2,1)S(1)} %get-tuple-element.13), channel_id=1, replica_groups=mesh['pool'=4,'ka'=32] {'pool','ka'}, dimensions={0} | all-to-all | bytes 6291456 | tf_op jit(solution)/shard_map/all_to_all | solution.py:290
  157.2 2.3 %step.1 = bf16[128,96,128]{2,1,0:T(8,128)(2,1)S(1)} custom-call(s32[128]{0:T(128)S(1)} %bitcast.10, bf16[128,96,128]{2,1,0:T(8,128)(2,1)S(1)} %all_to_all.16.x_ref, bf16[256,8192]{1,0:T(8,128)(2,1)S(1)} %get-tuple-element.14.op_ref, f32[4,96,128]{2,1,0:T(8,128)S(1)} %get-tuple-element.11.drive_ref, f32[4,96,128]{2,1,0:T(8,128)S(1)} %get-tuple-element.12.tau_ref), custom_call_target="tpu_custom_call" | custom-call | tf_op jit(solution)/shard_map/step/pallas_call | solution.py:282
  159.5 45.6 %all_to_all.17.x_ref = bf16[128,96,128]{2,1,0:T(8,128)(2,1)S(1)} all-to-all(bf16[128,96,128]{2,1,0:T(8,128)(2,1)S(1)} %step.1), channel_id=1, replica_groups=mesh['pool'=4,'ka'=32] {'pool','ka'}, dimensions={0} | all-to-all | bytes 6291456 | tf_op jit(solution)/shard_map/all_to_all | solution.py:290
  205.1 2.6 %step_last.1 = f32[4,12288]{1,0:T(4,128)} custom-call(s32[128]{0:T(128)S(1)} %bitcast.11, bf16[128,96,128]{2,1,0:T(8,128)(2,1)S(1)} %all_to_all.17.x_ref, bf16[256,8192]{1,0:T(8,128)(2,1)S(1)} %get-tuple-element.14.op_ref, f32[4,96,128]{2,1,0:T(8,128)S(1)} %get-tuple-element.11.drive_ref, f32[4,96,128]{2,1,0:T(8,128)S(1)} %get-tuple-element.12.tau_ref), custom_call_target="tpu_custom_call" | custom-call | tf_op jit(solution)/shard_map/step_last/pallas_call | solution.py:282
Async XLA Ops:
  0.0 2.2 %copy-start.3 = (s32[256,1]{0,1:T(1,128)S(1)}, s32[256,1]{0,1:T(1,128)}, u32[]{:S(2)}) copy-start(s32[256,1]{0,1:T(1,128)} %param.8) | copy-start | bytes 3076
  0.0 2.2 %copy-start.1 = (f32[4,4096]{1,0:T(4,128)S(1)}, f32[4,4096]{1,0:T(4,128)}, u32[]{:S(2)}) copy-start(f32[4,4096]{1,0:T(4,128)} %tau_ref.1) | copy-start | bytes 196612
  0.0 2.2 %copy-start = (f32[4,12288]{1,0:T(4,128)S(1)}, f32[4,12288]{1,0:T(4,128)}, u32[]{:S(2)}) copy-start(f32[4,12288]{1,0:T(4,128)} %drive_ref.1) | copy-start | bytes 589828
  0.0 2.2 %copy-start.2 = (s32[1,128]{1,0:T(1,128)S(1)}, s32[1,128]{1,0:T(1,128)}, u32[]{:S(2)}) copy-start(s32[1,128]{1,0:T(1,128)} %param.11) | copy-start | bytes 1540
  0.0 2.2 %copy-start.5 = (s32[256]{0:T(256)S(1)}, s32[256]{0:T(256)}, u32[]{:S(2)}) copy-start(s32[256]{0:T(256)} %param.10) | copy-start | bytes 3076
  0.0 2.2 %copy-start.4 = (s32[256]{0:T(256)S(1)}, s32[256]{0:T(256)}, u32[]{:S(2)}) copy-start(s32[256]{0:T(256)} %param.9) | copy-start | bytes 3076
